TPU v7x, 32 devices: a whole 2x2x4 slice. The times are simulated.
32 devices in a mesh: grp: 2 (over y), row: 4 (over z), col: 4 (over x, core).
Axes of the slice: x: 2, y: 2, z: 4, core: 2. Of those that a mesh axis runs over, the one named last changes fastest.
Arguments:
- mask_param: float32 [2048, 1024], P(('grp', 'row'), 'col'), parts along dimension 0, may hold values from -6 to 6
- target: bfloat16 [2048, 1024], P(('grp', 'row'), 'col'), parts along dimension 0, may hold values from 0 to 1
- kernel_modes: float32 [12, 64, 128], replicated, may hold values from -24 to 24, as said below
- kernel_weight: float32 [12], replicated, may hold values from 0.02 to 0.2
Outputs:
- healed_param: float32 [2048, 1024], P(('grp', 'row'), 'col'), parts along dimension 0
There are 2 independent parts, one for each index of `grp`. A program takes and returns all parts, laid end to end along the dimension named above; an argument that names none is the same for every part. Nothing has to cross between parts.
Inputs may be any that keep to these rules, and one draw needn't show every extreme that they name: `kernel_modes`: the response of every kernel at the zero-frequency mode (row 32, columns 32 and 96) is zero.
All inputs are finite; a program needn't handle non-finite values.
Results may differ from a plain program's by a relative error of at most 0.0095.
Values may be sent and summed in bfloat16 or wider, within the bound.
No kernel may reach another device: no remote copies, remote signals or barrier semaphores. Data moves between devices by JAX's collectives and lax.ppermute only.
A program may use at most 64 MiB of HBM per device.

v0:
```python
import math

import jax
import jax.numpy as jnp
from jax import lax
from jax.sharding import PartitionSpec as P

TILE = 256
MARGIN = 64
MODES = 64
KERN = 12
HALF = 128
WIN = 384


steepness = 4.0
threshold = 0.4
step_rate = 16.0


def with_halo(block, sides, width):
    for axis, dim in sides:
        count = lax.axis_size(axis)
        forward = [(i, i + 1) for i in range(count - 1)]
        backward = [(target, source) for source, target in forward]
        low = lax.ppermute(
            lax.slice_in_dim(block, block.shape[dim] - width, None, axis=dim), axis, forward
        )
        high = lax.ppermute(lax.slice_in_dim(block, 0, width, axis=dim), axis, backward)
        block = jnp.concatenate([low, block, high], axis=dim)
    return block


def shifted(block, axis, distance):
    devices = range(lax.axis_size(axis))
    route = [(i - distance, i) for i in devices if i - distance in devices]
    return lax.ppermute(block, axis, route)


def dft_tables():
    frequency = jnp.arange(MODES, dtype=jnp.int32) - MODES // 2
    places = jnp.arange(WIN, dtype=jnp.int32)
    phase_index = jnp.mod(frequency[:, None] * places[None, :], WIN)
    phase_angle = phase_index.astype(jnp.float32) * (2.0 * math.pi / WIN)
    cos_table = jnp.cos(phase_angle).astype(jnp.bfloat16)
    sin_table = jnp.sin(phase_angle).astype(jnp.bfloat16)
    stacked = jnp.concatenate([cos_table, sin_table], axis=0)
    forward_table = jnp.concatenate([cos_table.T, sin_table.T], axis=1)
    inverse_table = jnp.concatenate(
        [jnp.concatenate([cos_table, sin_table], 1), jnp.concatenate([-sin_table, cos_table], 1)], 0
    )
    adjoint_table = jnp.concatenate(
        [
            jnp.concatenate([cos_table.T, -sin_table.T], 1),
            jnp.concatenate([sin_table.T, cos_table.T], 1),
        ],
        0,
    )
    return (stacked, forward_table, inverse_table, adjoint_table)


def window_gradient(window_mask, target_core, weight_core, kernel_modes, kernel_weight, tables):
    stacked, forward_table, inverse_table, adjoint_table = tables
    half_spec = jnp.dot(window_mask, forward_table, preferred_element_type=jnp.float32).astype(
        jnp.bfloat16
    )
    blocks = jnp.dot(stacked, half_spec, preferred_element_type=jnp.float32)
    spec_real = (blocks[:MODES, :MODES] - blocks[MODES:, MODES:]) / (WIN * WIN)
    spec_imag = -(blocks[:MODES, MODES:] + blocks[MODES:, :MODES]) / (WIN * WIN)
    kernel_pairs = KERN // 2
    mode_pairs = kernel_modes.reshape(kernel_pairs, 2, MODES, 2 * MODES)
    weight_pairs = kernel_weight.reshape(kernel_pairs, 2)

    def spread(kernel_pair):
        resp_real = kernel_pair[:, :, :MODES]
        resp_imag = kernel_pair[:, :, MODES:]
        filtered = jnp.concatenate(
            [
                resp_real * spec_real - resp_imag * spec_imag,
                resp_real * spec_imag + resp_imag * spec_real,
            ],
            2,
        ).astype(jnp.bfloat16)
        return jnp.einsum(
            "kfg,gh->kfh", filtered, inverse_table, preferred_element_type=jnp.float32
        ).astype(jnp.bfloat16)

    def fields(partial_value):
        field_real = partial_value[:, :, :WIN]
        field_imag = partial_value[:, :, WIN:]
        rotated = jnp.concatenate(
            [
                jnp.concatenate([field_real, field_imag], 2),
                jnp.concatenate([-field_imag, field_real], 2),
            ],
            1,
        )
        return jnp.einsum("fx,kfh->kxh", stacked, rotated, preferred_element_type=jnp.float32)

    def add_intensity(running, inputs):
        kernel_pair, weights = inputs
        partial_value = spread(kernel_pair)
        field_pair = fields(partial_value)
        field_power = (
            field_pair[:, :, :WIN] * field_pair[:, :, :WIN]
            + field_pair[:, :, WIN:] * field_pair[:, :, WIN:]
        )
        return (running + jnp.sum(weights[:, None, None] * field_power, axis=0), partial_value)

    intensity, partials = lax.scan(
        add_intensity, jnp.zeros((WIN, WIN), jnp.float32), (mode_pairs, weight_pairs)
    )
    core_level = intensity[MARGIN : MARGIN + TILE, MARGIN : MARGIN + TILE]
    printed = jax.nn.sigmoid(steepness * (core_level - threshold))
    core_grad = (
        2.0
        * (printed - target_core.astype(jnp.float32))
        * printed
        * (1.0 - printed)
        * steepness
        * weight_core
    )
    grad_full = jnp.pad(core_grad, MARGIN)
    grad_both = jnp.concatenate([grad_full, grad_full], 1)

    def add_adjoint(running, inputs):
        kernel_pair, weights, partial_value = inputs
        field_pair = fields(partial_value)
        scaled = (field_pair * grad_both[None] * (2.0 * weights)[:, None, None]).astype(
            jnp.bfloat16
        )
        half_back = jnp.einsum(
            "kxh,hf->kxf", scaled, adjoint_table, preferred_element_type=jnp.float32
        ).astype(jnp.bfloat16)
        back_modes = jnp.einsum(
            "gx,kxf->kgf", stacked, half_back, preferred_element_type=jnp.float32
        )
        back_real = back_modes[:, :MODES, :MODES] + back_modes[:, MODES:, MODES:]
        back_imag = back_modes[:, :MODES, MODES:] - back_modes[:, MODES:, :MODES]
        resp_real = kernel_pair[:, :, :MODES]
        resp_imag = kernel_pair[:, :, MODES:]
        new_real = running[0] + jnp.sum(resp_real * back_real + resp_imag * back_imag, axis=0)
        new_imag = running[1] + jnp.sum(resp_real * back_imag - resp_imag * back_real, axis=0)
        return ((new_real, new_imag), None)

    zero_modes = jnp.zeros((MODES, MODES), jnp.float32)
    (acc_real, acc_imag), _ = lax.scan(
        add_adjoint, (zero_modes, zero_modes), (mode_pairs, weight_pairs, partials)
    )
    combined = jnp.concatenate([acc_real, acc_imag], 1).astype(jnp.bfloat16)
    partial_back = jnp.dot(combined, inverse_table, preferred_element_type=jnp.float32).astype(
        jnp.bfloat16
    )
    stacked_back = jnp.concatenate([partial_back[:, :WIN], -partial_back[:, WIN:]], 0)
    mask_grad = jnp.einsum(
        "fx,fy->xy", stacked, stacked_back, preferred_element_type=jnp.float32
    ) / (WIN * WIN)
    return mask_grad[MARGIN : MARGIN + TILE, MARGIN : MARGIN + TILE]


def heal_from_param(
    heal_param, heal_goal, inside, core_weight, kernel_modes, kernel_weight, tables
):
    heal_wire = jnp.where(inside, jax.nn.sigmoid(heal_param), 0.0).astype(jnp.bfloat16)
    heal_grad = window_gradient(
        heal_wire, heal_goal, core_weight, kernel_modes, kernel_weight, tables
    )
    core_param = heal_param[MARGIN : MARGIN + TILE, MARGIN : MARGIN + TILE]
    core_soft = jax.nn.sigmoid(core_param)
    return core_param - step_rate * (heal_grad * core_soft * (1.0 - core_soft))


def per_device(mask_param, target, kernel_modes, kernel_weight):
    row_pos = lax.axis_index("row")
    col_pos = lax.axis_index("col")
    row_count = lax.axis_size("row")
    col_count = lax.axis_size("col")
    tables = dft_tables()
    soft_mask = jax.nn.sigmoid(mask_param)
    wire_mask = soft_mask.astype(jnp.bfloat16)
    window = with_halo(wire_mask, (("row", 0), ("col", 1)), MARGIN)
    unit_weight = jnp.ones((TILE, TILE), jnp.float32)
    mask_grad = window_gradient(window, target, unit_weight, kernel_modes, kernel_weight, tables)
    first_param = mask_param - step_rate * (mask_grad * soft_mask * (1.0 - soft_mask))
    rim_reach = HALF + MARGIN
    window_place = jnp.arange(WIN, dtype=jnp.int32) + (HALF - MARGIN)
    rows_in = row_pos * TILE + window_place < row_count * TILE
    cols_in = col_pos * TILE + window_place < col_count * TILE
    inside = rows_in[:, None] & cols_in[None, :]
    core_weight = inside[MARGIN : MARGIN + TILE, MARGIN : MARGIN + TILE].astype(jnp.float32)
    from_right = (
        shifted(first_param[:, :rim_reach], "col", -1),
        shifted(target[:, :HALF].astype(jnp.float32), "col", -1).astype(jnp.bfloat16),
    )
    cols_param = jnp.concatenate([first_param[:, HALF - MARGIN :], from_right[0]], 1)
    cols_goal = jnp.concatenate([target[:, HALF:], from_right[1]], 1)
    from_below = (
        shifted(cols_param[:rim_reach], "row", -1),
        shifted(cols_goal[:HALF].astype(jnp.float32), "row", -1).astype(jnp.bfloat16),
    )
    heal_param = jnp.concatenate([cols_param[HALF - MARGIN :], from_below[0]], 0)
    heal_goal = jnp.concatenate([cols_goal[HALF:], from_below[1]], 0)
    returned = heal_from_param(
        heal_param, heal_goal, inside, core_weight, kernel_modes, kernel_weight, tables
    )
    lead_rows = TILE - HALF
    to_right = shifted(returned[:, lead_rows:], "col", 1)
    col_full = jnp.concatenate([to_right, returned[:, :lead_rows]], 1)
    to_below = shifted(col_full[lead_rows:], "row", 1)
    assembled = jnp.concatenate([to_below, col_full[:lead_rows]], 0)
    local_index = jnp.arange(TILE, dtype=jnp.int32)
    rows_done = (local_index >= HALF) | (row_pos >= 1)
    cols_done = (local_index >= HALF) | (col_pos >= 1)
    return jnp.where(rows_done[:, None] & cols_done[None, :], assembled, first_param)


def solution(mesh):
    in_specs = (P(("grp", "row"), "col"), P(("grp", "row"), "col"), P(), P())
    out_specs = P(("grp", "row"), "col")
    return jax.shard_map(
        per_device, mesh=mesh, in_specs=in_specs, out_specs=out_specs, check_vma=False
    )
```

profile of v0, /device:TPU:10, one launch (start us, length us, event | category | flops | bytes accessed | tf_op | source)
XLA Modules:
  0.0 136.6 jit_solution(1431372960824281353)
XLA Ops:
  0.0 1.1 copy.50
  1.3 3.5 %collective-permute-start = (bf16[64,256]{0,1:T(8,128)(2,1)S(1)}, bf16[64,256]{0,1:T(8,128)(2,1)S(1)}, u32[]{:S(2)}, u32[]{:S(2)}) collective-permute-start(bf16[64,256]{0,1:T(8,128)(2,1)S(1)} %get-tuple-element.541), channel_id=1, source_target_pairs={{0,4},{4,8},{8,12},{1,5},{5,9},{9,13},{2,6},{6,10},{10,14},{3,7},{... | collective-permute-start | bytes 98312 | tf_op jit(solution)/shard_map/ppermute | solution.py:26
  4.8 2.4 %collective-permute-start.1 = (bf16[64,256]{0,1:T(8,128)(2,1)S(1)}, bf16[64,256]{0,1:T(8,128)(2,1)S(1)}, u32[]{:S(2)}, u32[]{:S(2)}) collective-permute-start(bf16[64,256]{0,1:T(8,128)(2,1)S(1)} %get-tuple-element.542), channel_id=1, source_target_pairs={{4,0},{8,4},{12,8},{5,1},{9,5},{13,9},{6,2},{10,6},{14,10},{7,3},{... | collective-permute-start | bytes 98312 | tf_op jit(solution)/shard_map/ppermute | solution.py:29
  7.7 0.8 cosine_convert_fusion
  9.8 0.8 maximum_maximum_fusion.1
  11.1 1.9 %collective-permute-start.2 = (bf16[384,64]{0,1:T(8,128)(2,1)S(1)}, bf16[384,64]{0,1:T(8,128)(2,1)S(1)}, u32[]{:S(2)}, u32[]{:S(2)}) collective-permute-start(bf16[384,64]{0,1:T(8,128)(2,1)S(1)} %get-tuple-element.535), channel_id=1, source_target_pairs={{0,1},{1,2},{2,3},{4,5},{5,6},{6,7},{8,9},{9,10},{10,11},{12,13},{... | collective-permute-start | bytes 147464 | tf_op jit(solution)/shard_map/ppermute | solution.py:26
  13.0 3.6 %collective-permute-start.3 = (bf16[384,64]{0,1:T(8,128)(2,1)S(1)}, bf16[384,64]{0,1:T(8,128)(2,1)S(1)}, u32[]{:S(2)}, u32[]{:S(2)}) collective-permute-start(bf16[384,64]{0,1:T(8,128)(2,1)S(1)} %get-tuple-element.536), channel_id=1, source_target_pairs={{1,0},{2,1},{3,2},{5,4},{6,5},{7,6},{9,8},{10,9},{11,10},{13,12},{... | collective-permute-start | bytes 147464 | tf_op jit(solution)/shard_map/ppermute | solution.py:29
  17.6 1.3 copy.45
  20.3 17.6 %while.52 = (s32[]{:T(128)}, f32[384,384]{0,1:T(8,128)S(1)}, bf16[6,2,64,768]{3,2,1,0:T(8,128)(2,1)S(1)}, f32[6,2]{1,0:T(8,128)S(1)}, f32[6,2,64,128]{3,2,1,0:T(...) while((s32[]{:T(128)}, f32[384,384]{0,1:T(8,128)S(1)}, ...), condition=%wide.region_2.3_spmd.clone, body=%wide.region_0.2_spmd.clone.sunk | while | flops 179240960 | bytes 8880283 | solution.py:110
  20.3 0.8 dynamic-slice_bitcast_fusion.8
  21.2 0.9 subtract_convert_fusion.4
  23.2 0.8 dynamic-slice_bitcast_fusion.8
  24.1 0.9 subtract_convert_fusion.4
  26.2 0.8 dynamic-slice_bitcast_fusion.8
  27.0 0.9 subtract_convert_fusion.4
  29.1 0.8 dynamic-slice_bitcast_fusion.8
  29.9 0.9 subtract_convert_fusion.4
  32.0 0.8 dynamic-slice_bitcast_fusion.8
  32.9 0.9 subtract_convert_fusion.4
  34.9 0.8 dynamic-slice_bitcast_fusion.8
  35.8 0.9 subtract_convert_fusion.4
  37.9 1.1 multiply_multiply_fusion
  39.2 1.1 pad_maximum_fusion
  40.3 18.8 %while.53 = (s32[]{:T(128)}, f32[64,64]{0,1:T(8,128)S(1)}, f32[64,64]{0,1:T(8,128)S(1)}, f32[6,2,64,128]{2,3,1,0:T(8,128)S(1)}, bf16[6,2,64,768]{3,2,1,0:T(8,128...) while((s32[]{:T(128)}, f32[64,64]{0,1:T(8,128)S(1)}, ...), condition=%wide.region_6.7_spmd.clone, body=%wide.region_3.6_spmd.clone.sunk | while | flops 330342400 | bytes 4128923 | solution.py:147
  40.6 2.4 %fusion.211 = bf16[2,384,128]{2,1,0:T(8,128)(2,1)S(1)} fusion(f32[2]{0:T(128)S(1)} %fusion.210, f32[384,768]{0,1:T(8,128)} %get-tuple-element.888, bf16[2,64,384]{1,2,0:T(8,128)(2,1)S(1)} %get-tuple-element.791, bf16[2,64,384]{1,2,0:T(8,128)(2,1)S(1)} %get-tuple-element.792, bf16[2,64,768]{1,2,0:T(8,128)(2,1)S(1)} %bitcast.150, ...), kind=kOutput, calls=%fused_computation.33.clone.1 | convolution fusion | flops 305037312 | bytes 2064392 | tf_op jit(solution)/shard_map/while/body/eval_jaxpr/kxh,hf->kxf/dot_general | solution.py:132
  43.7 2.4 %fusion.211 = bf16[2,384,128]{2,1,0:T(8,128)(2,1)S(1)} fusion(f32[2]{0:T(128)S(1)} %fusion.210, f32[384,768]{0,1:T(8,128)} %get-tuple-element.888, bf16[2,64,384]{1,2,0:T(8,128)(2,1)S(1)} %get-tuple-element.791, bf16[2,64,384]{1,2,0:T(8,128)(2,1)S(1)} %get-tuple-element.792, bf16[2,64,768]{1,2,0:T(8,128)(2,1)S(1)} %bitcast.150, ...), kind=kOutput, calls=%fused_computation.33.clone.1 | convolution fusion | flops 305037312 | bytes 2064392 | tf_op jit(solution)/shard_map/while/body/eval_jaxpr/kxh,hf->kxf/dot_general | solution.py:132
  46.9 2.4 %fusion.211 = bf16[2,384,128]{2,1,0:T(8,128)(2,1)S(1)} fusion(f32[2]{0:T(128)S(1)} %fusion.210, f32[384,768]{0,1:T(8,128)} %get-tuple-element.888, bf16[2,64,384]{1,2,0:T(8,128)(2,1)S(1)} %get-tuple-element.791, bf16[2,64,384]{1,2,0:T(8,128)(2,1)S(1)} %get-tuple-element.792, bf16[2,64,768]{1,2,0:T(8,128)(2,1)S(1)} %bitcast.150, ...), kind=kOutput, calls=%fused_computation.33.clone.1 | convolution fusion | flops 305037312 | bytes 2064392 | tf_op jit(solution)/shard_map/while/body/eval_jaxpr/kxh,hf->kxf/dot_general | solution.py:132
  50.0 2.4 %fusion.211 = bf16[2,384,128]{2,1,0:T(8,128)(2,1)S(1)} fusion(f32[2]{0:T(128)S(1)} %fusion.210, f32[384,768]{0,1:T(8,128)} %get-tuple-element.888, bf16[2,64,384]{1,2,0:T(8,128)(2,1)S(1)} %get-tuple-element.791, bf16[2,64,384]{1,2,0:T(8,128)(2,1)S(1)} %get-tuple-element.792, bf16[2,64,768]{1,2,0:T(8,128)(2,1)S(1)} %bitcast.150, ...), kind=kOutput, calls=%fused_computation.33.clone.1 | convolution fusion | flops 305037312 | bytes 2064392 | tf_op jit(solution)/shard_map/while/body/eval_jaxpr/kxh,hf->kxf/dot_general | solution.py:132
  53.1 2.4 %fusion.211 = bf16[2,384,128]{2,1,0:T(8,128)(2,1)S(1)} fusion(f32[2]{0:T(128)S(1)} %fusion.210, f32[384,768]{0,1:T(8,128)} %get-tuple-element.888, bf16[2,64,384]{1,2,0:T(8,128)(2,1)S(1)} %get-tuple-element.791, bf16[2,64,384]{1,2,0:T(8,128)(2,1)S(1)} %get-tuple-element.792, bf16[2,64,768]{1,2,0:T(8,128)(2,1)S(1)} %bitcast.150, ...), kind=kOutput, calls=%fused_computation.33.clone.1 | convolution fusion | flops 305037312 | bytes 2064392 | tf_op jit(solution)/shard_map/while/body/eval_jaxpr/kxh,hf->kxf/dot_general | solution.py:132
  56.3 2.4 %fusion.211 = bf16[2,384,128]{2,1,0:T(8,128)(2,1)S(1)} fusion(f32[2]{0:T(128)S(1)} %fusion.210, f32[384,768]{0,1:T(8,128)} %get-tuple-element.888, bf16[2,64,384]{1,2,0:T(8,128)(2,1)S(1)} %get-tuple-element.791, bf16[2,64,384]{1,2,0:T(8,128)(2,1)S(1)} %get-tuple-element.792, bf16[2,64,768]{1,2,0:T(8,128)(2,1)S(1)} %bitcast.150, ...), kind=kOutput, calls=%fused_computation.33.clone.1 | convolution fusion | flops 305037312 | bytes 2064392 | tf_op jit(solution)/shard_map/while/body/eval_jaxpr/kxh,hf->kxf/dot_general | solution.py:132
  60.2 3.3 %collective-permute-start.4 = (f32[256,192]{0,1:T(8,128)S(1)}, f32[256,192]{0,1:T(8,128)S(1)}, u32[]{:S(2)}, u32[]{:S(2)}) collective-permute-start(f32[256,192]{0,1:T(8,128)S(1)} %get-tuple-element.534), channel_id=1, source_target_pairs={{1,0},{2,1},{3,2},{5,4},{6,5},{7,6},{9,8},{10,9},{11,10},{13,12},{... | collective-permute-start | bytes 589832 | tf_op jit(solution)/shard_map/ppermute | solution.py:37
  64.2 1.9 %collective-permute-start.6 = (bf16[256,128]{0,1:T(8,128)(2,1)}, bf16[256,128]{0,1:T(8,128)(2,1)}, u32[]{:S(2)}, u32[]{:S(2)}) collective-permute-start(bf16[256,128]{0,1:T(8,128)(2,1)} %get-tuple-element.540), channel_id=1, source_target_pairs={{1,0},{2,1},{3,2},{5,4},{6,5},{7,6},{9,8},{10,9},{11,10},{13,12},{... | collective-permute-start | bytes 196616 | tf_op jit(solution)/shard_map/ppermute | solution.py:37
  66.9 2.4 %collective-permute-start.5 = (f32[192,384]{0,1:T(8,128)S(1)}, f32[192,384]{0,1:T(8,128)S(1)}, u32[]{:S(2)}, u32[]{:S(2)}) collective-permute-start(f32[192,384]{0,1:T(8,128)S(1)} %get-tuple-element.530), channel_id=1, source_target_pairs={{4,0},{8,4},{12,8},{5,1},{9,5},{13,9},{6,2},{10,6},{14,10},{7,3},{... | collective-permute-start | bytes 884744 | tf_op jit(solution)/shard_map/ppermute | solution.py:37
  69.3 0.8 broadcast_and_fusion
  70.1 1.4 %fusion.139 = (bf16[128,256]{0,1:T(8,128)(2,1)}, bf16[128,256]{0,1:T(8,128)(2,1)}) fusion(bf16[256,128]{0,1:T(8,128)(2,1)S(1)} %get-tuple-element.539, bf16[256,128]{0,1:T(8,128)(2,1)} %collective-permute-done.6), kind=kLoop, calls=%fused_computation.194 | loop fusion | flops 262144 | bytes 262144 | tf_op jit(solution)/shard_map/concatenate | solution.py:196
  71.5 2.1 %collective-permute-start.7 = (bf16[128,256]{0,1:T(8,128)(2,1)}, bf16[128,256]{0,1:T(8,128)(2,1)}, u32[]{:S(2)}, u32[]{:S(2)}) collective-permute-start(bf16[128,256]{0,1:T(8,128)(2,1)} %get-tuple-element.538), channel_id=1, source_target_pairs={{4,0},{8,4},{12,8},{5,1},{9,5},{13,9},{6,2},{10,6},{14,10},{7,3},{... | collective-permute-start | bytes 196616 | tf_op jit(solution)/shard_map/ppermute | solution.py:37
  73.6 7.2 %collective-permute-done.5 = f32[192,384]{0,1:T(8,128)S(1)} collective-permute-done((f32[192,384]{0,1:T(8,128)S(1)}, f32[192,384]{0,1:T(8,128)S(1)}, u32[]{:S(2)}, u32[]{:S(2)}) %collective-permute-start.5) | collective-permute-done | bytes 294944 | tf_op jit(solution)/shard_map/ppermute | solution.py:37
  82.3 17.6 %while.54 = (s32[]{:T(128)}, f32[384,384]{0,1:T(8,128)S(1)}, bf16[6,2,64,768]{3,2,1,0:T(8,128)(2,1)S(1)}, f32[6,2]{1,0:T(8,128)S(1)}, f32[6,2,64,128]{3,2,1,0:T(...) while((s32[]{:T(128)}, f32[384,384]{0,1:T(8,128)S(1)}, ...), condition=%wide.region_9.10_spmd.clone, body=%wide.region_7.9_spmd.clone.sunk | while | flops 179240960 | bytes 8880283 | solution.py:110
  82.3 0.8 dynamic-slice_bitcast_fusion.10
  83.2 0.9 subtract_convert_fusion.5
  85.3 0.8 dynamic-slice_bitcast_fusion.10
  86.1 0.9 subtract_convert_fusion.5
  88.2 0.8 dynamic-slice_bitcast_fusion.10
  89.0 0.9 subtract_convert_fusion.5
  91.1 0.8 dynamic-slice_bitcast_fusion.10
  92.0 0.9 subtract_convert_fusion.5
  94.1 0.8 dynamic-slice_bitcast_fusion.10
  94.9 0.9 subtract_convert_fusion.5
  97.0 0.8 dynamic-slice_bitcast_fusion.10
  97.8 0.9 subtract_convert_fusion.5
  99.9 1.1 multiply_select_fusion
  101.3 1.1 pad_maximum_fusion.1
  102.4 18.7 %while.55 = (s32[]{:T(128)}, f32[64,64]{0,1:T(8,128)S(1)}, f32[64,64]{0,1:T(8,128)S(1)}, f32[6,2,64,128]{2,3,1,0:T(8,128)S(1)}, bf16[6,2,64,768]{3,2,1,0:T(8,128...) while((s32[]{:T(128)}, f32[64,64]{0,1:T(8,128)S(1)}, ...), condition=%wide.region_13.14_spmd.clone, body=%wide.region_10.13_spmd.clone.sunk | while | flops 330342400 | bytes 4128923 | solution.py:147
  102.7 2.4 %fusion.222 = bf16[2,384,128]{2,1,0:T(8,128)(2,1)S(1)} fusion(f32[2]{0:T(128)S(1)} %fusion.221, f32[384,768]{0,1:T(8,128)} %get-tuple-element.954, bf16[2,64,384]{1,2,0:T(8,128)(2,1)S(1)} %get-tuple-element.821, bf16[2,64,384]{1,2,0:T(8,128)(2,1)S(1)} %get-tuple-element.822, bf16[2,64,768]{1,2,0:T(8,128)(2,1)S(1)} %bitcast.152, ...), kind=kOutput, calls=%fused_computation.89.clone.1 | convolution fusion | flops 305037312 | bytes 2064392 | tf_op jit(solution)/shard_map/while/body/eval_jaxpr/kxh,hf->kxf/dot_general | solution.py:132
  105.9 2.4 %fusion.222 = bf16[2,384,128]{2,1,0:T(8,128)(2,1)S(1)} fusion(f32[2]{0:T(128)S(1)} %fusion.221, f32[384,768]{0,1:T(8,128)} %get-tuple-element.954, bf16[2,64,384]{1,2,0:T(8,128)(2,1)S(1)} %get-tuple-element.821, bf16[2,64,384]{1,2,0:T(8,128)(2,1)S(1)} %get-tuple-element.822, bf16[2,64,768]{1,2,0:T(8,128)(2,1)S(1)} %bitcast.152, ...), kind=kOutput, calls=%fused_computation.89.clone.1 | convolution fusion | flops 305037312 | bytes 2064392 | tf_op jit(solution)/shard_map/while/body/eval_jaxpr/kxh,hf->kxf/dot_general | solution.py:132
  109.0 2.4 %fusion.222 = bf16[2,384,128]{2,1,0:T(8,128)(2,1)S(1)} fusion(f32[2]{0:T(128)S(1)} %fusion.221, f32[384,768]{0,1:T(8,128)} %get-tuple-element.954, bf16[2,64,384]{1,2,0:T(8,128)(2,1)S(1)} %get-tuple-element.821, bf16[2,64,384]{1,2,0:T(8,128)(2,1)S(1)} %get-tuple-element.822, bf16[2,64,768]{1,2,0:T(8,128)(2,1)S(1)} %bitcast.152, ...), kind=kOutput, calls=%fused_computation.89.clone.1 | convolution fusion | flops 305037312 | bytes 2064392 | tf_op jit(solution)/shard_map/while/body/eval_jaxpr/kxh,hf->kxf/dot_general | solution.py:132
  112.1 2.4 %fusion.222 = bf16[2,384,128]{2,1,0:T(8,128)(2,1)S(1)} fusion(f32[2]{0:T(128)S(1)} %fusion.221, f32[384,768]{0,1:T(8,128)} %get-tuple-element.954, bf16[2,64,384]{1,2,0:T(8,128)(2,1)S(1)} %get-tuple-element.821, bf16[2,64,384]{1,2,0:T(8,128)(2,1)S(1)} %get-tuple-element.822, bf16[2,64,768]{1,2,0:T(8,128)(2,1)S(1)} %bitcast.152, ...), kind=kOutput, calls=%fused_computation.89.clone.1 | convolution fusion | flops 305037312 | bytes 2064392 | tf_op jit(solution)/shard_map/while/body/eval_jaxpr/kxh,hf->kxf/dot_general | solution.py:132
  115.2 2.4 %fusion.222 = bf16[2,384,128]{2,1,0:T(8,128)(2,1)S(1)} fusion(f32[2]{0:T(128)S(1)} %fusion.221, f32[384,768]{0,1:T(8,128)} %get-tuple-element.954, bf16[2,64,384]{1,2,0:T(8,128)(2,1)S(1)} %get-tuple-element.821, bf16[2,64,384]{1,2,0:T(8,128)(2,1)S(1)} %get-tuple-element.822, bf16[2,64,768]{1,2,0:T(8,128)(2,1)S(1)} %bitcast.152, ...), kind=kOutput, calls=%fused_computation.89.clone.1 | convolution fusion | flops 305037312 | bytes 2064392 | tf_op jit(solution)/shard_map/while/body/eval_jaxpr/kxh,hf->kxf/dot_general | solution.py:132
  118.3 2.4 %fusion.222 = bf16[2,384,128]{2,1,0:T(8,128)(2,1)S(1)} fusion(f32[2]{0:T(128)S(1)} %fusion.221, f32[384,768]{0,1:T(8,128)} %get-tuple-element.954, bf16[2,64,384]{1,2,0:T(8,128)(2,1)S(1)} %get-tuple-element.821, bf16[2,64,384]{1,2,0:T(8,128)(2,1)S(1)} %get-tuple-element.822, bf16[2,64,768]{1,2,0:T(8,128)(2,1)S(1)} %bitcast.152, ...), kind=kOutput, calls=%fused_computation.89.clone.1 | convolution fusion | flops 305037312 | bytes 2064392 | tf_op jit(solution)/shard_map/while/body/eval_jaxpr/kxh,hf->kxf/dot_general | solution.py:132
  122.5 1.9 %collective-permute-start.8 = (f32[256,128]{0,1:T(8,128)S(1)}, f32[256,128]{0,1:T(8,128)S(1)}, u32[]{:S(2)}, u32[]{:S(2)}) collective-permute-start(f32[256,128]{0,1:T(8,128)S(1)} %get-tuple-element.531), channel_id=1, source_target_pairs={{0,1},{1,2},{2,3},{4,5},{5,6},{6,7},{8,9},{9,10},{10,11},{12,13},{... | collective-permute-start | bytes 393224 | tf_op jit(solution)/shard_map/ppermute | solution.py:37
  124.4 4.4 %collective-permute-done.8 = f32[256,128]{0,1:T(8,128)S(1)} collective-permute-done((f32[256,128]{0,1:T(8,128)S(1)}, f32[256,128]{0,1:T(8,128)S(1)}, u32[]{:S(2)}, u32[]{:S(2)}) %collective-permute-start.8) | collective-permute-done | bytes 131104 | tf_op jit(solution)/shard_map/ppermute | solution.py:37
  128.8 3.5 %collective-permute-start.9 = (f32[128,256]{0,1:T(8,128)S(1)}, f32[128,256]{0,1:T(8,128)S(1)}, u32[]{:S(2)}, u32[]{:S(2)}) collective-permute-start(f32[128,256]{0,1:T(8,128)S(1)} %fusion.125), channel_id=1, source_target_pairs={{0,4},{4,8},{8,12},{1,5},{5,9},{9,13},{2,6},{6,10},{10,14},{3,7},{... | collective-permute-start | bytes 393224 | tf_op jit(solution)/shard_map/ppermute | solution.py:37
  132.3 3.4 %collective-permute-done.9 = f32[128,256]{0,1:T(8,128)S(1)} collective-permute-done((f32[128,256]{0,1:T(8,128)S(1)}, f32[128,256]{0,1:T(8,128)S(1)}, u32[]{:S(2)}, u32[]{:S(2)}) %collective-permute-start.9) | collective-permute-done | bytes 131104 | tf_op jit(solution)/shard_map/ppermute | solution.py:37
  135.8 0.8 copy.55
  (266 shorter events, 32.4 us)
Async XLA Ops:
  1.1 15.6 %copy-start.2 = (f32[256,256]{0,1:T(8,128)}, f32[256,256]{0,1:T(8,128)S(1)}, u32[]{:S(2)}) copy-start(f32[256,256]{0,1:T(8,128)S(1)} %copy.50) | copy-start | bytes 786436
  1.1 15.6 %copy-start.22 = (f32[12]{0:T(128)S(1)}, f32[12]{0:T(128)}, u32[]{:S(2)}) copy-start(f32[12]{0:T(128)} %param.15) | copy-start | bytes 148
  1.1 15.7 %copy-start.21 = (bf16[256,256]{1,0:T(8,128)(2,1)S(1)}, bf16[256,256]{1,0:T(8,128)(2,1)}, u32[]{:S(2)}) copy-start(bf16[256,256]{1,0:T(8,128)(2,1)} %param.13) | copy-start | bytes 393220
  1.3 9.3 %collective-permute-start = (bf16[64,256]{0,1:T(8,128)(2,1)S(1)}, bf16[64,256]{0,1:T(8,128)(2,1)S(1)}, u32[]{:S(2)}, u32[]{:S(2)}) collective-permute-start(bf16[64,256]{0,1:T(8,128)(2,1)S(1)} %get-tuple-element.541), channel_id=1, source_target_pairs={{0,4},{4,8},{8,12},{1,5},{5,9},{9,13},{2,6},{6,10},{10,14},{3,7},{... | collective-permute-start | bytes 98312 | tf_op jit(solution)/shard_map/ppermute | solution.py:26
  4.8 6.2 %collective-permute-start.1 = (bf16[64,256]{0,1:T(8,128)(2,1)S(1)}, bf16[64,256]{0,1:T(8,128)(2,1)S(1)}, u32[]{:S(2)}, u32[]{:S(2)}) collective-permute-start(bf16[64,256]{0,1:T(8,128)(2,1)S(1)} %get-tuple-element.542), channel_id=1, source_target_pairs={{4,0},{8,4},{12,8},{5,1},{9,5},{13,9},{6,2},{10,6},{14,10},{7,3},{... | collective-permute-start | bytes 98312 | tf_op jit(solution)/shard_map/ppermute | solution.py:29
  8.5 10.4 %copy-start.13 = (bf16[384,64]{1,0:T(8,128)(2,1)}, bf16[384,64]{1,0:T(8,128)(2,1)S(1)}, u32[]{:S(2)}) copy-start(bf16[384,64]{1,0:T(8,128)(2,1)S(1)} %get-tuple-element.553) | copy-start | bytes 147460
  8.5 10.4 %copy-start.15 = (bf16[384,64]{1,0:T(8,128)(2,1)}, bf16[384,64]{1,0:T(8,128)(2,1)S(1)}, u32[]{:S(2)}) copy-start(bf16[384,64]{1,0:T(8,128)(2,1)S(1)} %get-tuple-element.554) | copy-start | bytes 147460
  9.0 7.8 %copy-start.18 = (bf16[64,384]{1,0:T(8,128)(2,1)}, bf16[64,384]{1,0:T(8,128)(2,1)S(1)}, u32[]{:S(2)}) copy-start(bf16[64,384]{1,0:T(8,128)(2,1)S(1)} %fusion.154) | copy-start | bytes 147460
  11.1 7.8 %collective-permute-start.2 = (bf16[384,64]{0,1:T(8,128)(2,1)S(1)}, bf16[384,64]{0,1:T(8,128)(2,1)S(1)}, u32[]{:S(2)}, u32[]{:S(2)}) collective-permute-start(bf16[384,64]{0,1:T(8,128)(2,1)S(1)} %get-tuple-element.535), channel_id=1, source_target_pairs={{0,1},{1,2},{2,3},{4,5},{5,6},{6,7},{8,9},{9,10},{10,11},{12,13},{... | collective-permute-start | bytes 147464 | tf_op jit(solution)/shard_map/ppermute | solution.py:26
  13.0 5.9 %collective-permute-start.3 = (bf16[384,64]{0,1:T(8,128)(2,1)S(1)}, bf16[384,64]{0,1:T(8,128)(2,1)S(1)}, u32[]{:S(2)}, u32[]{:S(2)}) collective-permute-start(bf16[384,64]{0,1:T(8,128)(2,1)S(1)} %get-tuple-element.536), channel_id=1, source_target_pairs={{1,0},{2,1},{3,2},{5,4},{6,5},{7,6},{9,8},{10,9},{11,10},{13,12},{... | collective-permute-start | bytes 147464 | tf_op jit(solution)/shard_map/ppermute | solution.py:29
  39.0 1.3 copy-start.9
  39.0 1.3 copy-start.10
  40.3 18.8 %copy-start.19 = (bf16[64,384]{1,0:T(8,128)(2,1)S(1)}, bf16[64,384]{1,0:T(8,128)(2,1)}, u32[]{:S(2)}) copy-start(bf16[64,384]{1,0:T(8,128)(2,1)} %copy-done.18) | copy-start | bytes 147460
  59.1 1.0 copy-start.3
  59.3 4.2 %copy-start.6 = (bf16[256,256]{0,1:T(8,128)(2,1)S(1)}, bf16[256,256]{0,1:T(8,128)(2,1)}, u32[]{:S(2)}) copy-start(bf16[256,256]{0,1:T(8,128)(2,1)} %copy.48) | copy-start | bytes 393220
  60.2 9.1 %copy-start = (f32[256,256]{0,1:T(8,128)}, f32[256,256]{0,1:T(8,128)S(1)}, u32[]{:S(2)}) copy-start(f32[256,256]{0,1:T(8,128)S(1)} %fusion.118) | copy-start | bytes 786436
  60.2 20.6 %copy-start.14 = (bf16[384,64]{1,0:T(8,128)(2,1)S(1)}, bf16[384,64]{1,0:T(8,128)(2,1)}, u32[]{:S(2)}) copy-start(bf16[384,64]{1,0:T(8,128)(2,1)} %copy-done.13) | copy-start | bytes 147460
  60.2 20.6 %copy-start.16 = (bf16[384,64]{1,0:T(8,128)(2,1)S(1)}, bf16[384,64]{1,0:T(8,128)(2,1)}, u32[]{:S(2)}) copy-start(bf16[384,64]{1,0:T(8,128)(2,1)} %copy-done.15) | copy-start | bytes 147460
  60.2 6.5 %collective-permute-start.4 = (f32[256,192]{0,1:T(8,128)S(1)}, f32[256,192]{0,1:T(8,128)S(1)}, u32[]{:S(2)}, u32[]{:S(2)}) collective-permute-start(f32[256,192]{0,1:T(8,128)S(1)} %get-tuple-element.534), channel_id=1, source_target_pairs={{1,0},{2,1},{3,2},{5,4},{6,5},{7,6},{9,8},{10,9},{11,10},{13,12},{... | collective-permute-start | bytes 589832 | tf_op jit(solution)/shard_map/ppermute | solution.py:37
  64.2 5.9 %collective-permute-start.6 = (bf16[256,128]{0,1:T(8,128)(2,1)}, bf16[256,128]{0,1:T(8,128)(2,1)}, u32[]{:S(2)}, u32[]{:S(2)}) collective-permute-start(bf16[256,128]{0,1:T(8,128)(2,1)} %get-tuple-element.540), channel_id=1, source_target_pairs={{1,0},{2,1},{3,2},{5,4},{6,5},{7,6},{9,8},{10,9},{11,10},{13,12},{... | collective-permute-start | bytes 196616 | tf_op jit(solution)/shard_map/ppermute | solution.py:37
  66.9 14.5 %copy-start.4 = (f32[192,384]{0,1:T(8,128)}, f32[192,384]{0,1:T(8,128)S(1)}, u32[]{:S(2)}) copy-start(f32[192,384]{0,1:T(8,128)S(1)} %get-tuple-element.529) | copy-start | bytes 884740
  66.9 13.9 %collective-permute-start.5 = (f32[192,384]{0,1:T(8,128)S(1)}, f32[192,384]{0,1:T(8,128)S(1)}, u32[]{:S(2)}, u32[]{:S(2)}) collective-permute-start(f32[192,384]{0,1:T(8,128)S(1)} %get-tuple-element.530), channel_id=1, source_target_pairs={{4,0},{8,4},{12,8},{5,1},{9,5},{13,9},{6,2},{10,6},{14,10},{7,3},{... | collective-permute-start | bytes 884744 | tf_op jit(solution)/shard_map/ppermute | solution.py:37
  71.5 28.4 %collective-permute-start.7 = (bf16[128,256]{0,1:T(8,128)(2,1)}, bf16[128,256]{0,1:T(8,128)(2,1)}, u32[]{:S(2)}, u32[]{:S(2)}) collective-permute-start(bf16[128,256]{0,1:T(8,128)(2,1)} %get-tuple-element.538), channel_id=1, source_target_pairs={{4,0},{8,4},{12,8},{5,1},{9,5},{13,9},{6,2},{10,6},{14,10},{7,3},{... | collective-permute-start | bytes 196616 | tf_op jit(solution)/shard_map/ppermute | solution.py:37
  80.8 0.7 copy-start.11
  101.1 1.3 copy-start.7
  101.1 1.3 copy-start.8
  101.1 1.3 copy-start.17
  102.4 18.8 %copy-start.20 = (bf16[64,384]{1,0:T(8,128)(2,1)S(1)}, bf16[64,384]{1,0:T(8,128)(2,1)}, u32[]{:S(2)}) copy-start(bf16[64,384]{1,0:T(8,128)(2,1)} %copy-done.18) | copy-start | bytes 147460
  121.1 1.0 copy-start.5
  121.1 1.1 copy-start.12
  122.3 13.4 %copy-start.1 = (f32[256,256]{0,1:T(8,128)S(1)}, f32[256,256]{0,1:T(8,128)}, u32[]{:S(2)}) copy-start(f32[256,256]{0,1:T(8,128)} %copy-done) | copy-start | bytes 786436
  122.5 6.3 %collective-permute-start.8 = (f32[256,128]{0,1:T(8,128)S(1)}, f32[256,128]{0,1:T(8,128)S(1)}, u32[]{:S(2)}, u32[]{:S(2)}) collective-permute-start(f32[256,128]{0,1:T(8,128)S(1)} %get-tuple-element.531), channel_id=1, source_target_pairs={{0,1},{1,2},{2,3},{4,5},{5,6},{6,7},{8,9},{9,10},{10,11},{12,13},{... | collective-permute-start | bytes 393224 | tf_op jit(solution)/shard_map/ppermute | solution.py:37
  128.8 6.9 %collective-permute-start.9 = (f32[128,256]{0,1:T(8,128)S(1)}, f32[128,256]{0,1:T(8,128)S(1)}, u32[]{:S(2)}, u32[]{:S(2)}) collective-permute-start(f32[128,256]{0,1:T(8,128)S(1)} %fusion.125), channel_id=1, source_target_pairs={{0,4},{4,8},{8,12},{1,5},{5,9},{9,13},{2,6},{6,10},{10,14},{3,7},{... | collective-permute-start | bytes 393224 | tf_op jit(solution)/shard_map/ppermute | solution.py:37
where the time goes:
time: 139 us; the launch traced here: 137 us
  matrix products  42.5 us (31%)
  other arithmetic  29.5 us (21%)
  starting transfers between devices  26.5 us (19%)
  local copies, waits for them, and re-layouts  19.9 us (14%)
  waiting for transfers between devices  15.8 us (11%)
  loops' own time  1.8 us (1%)
    dot_general x12, matrix products, add_adjoint(): jnp.einsum('kxh,hf->kxf', scaled, adjoint_table, preferred_element_type=j...  28.4 us
    ppermute x6, waiting for transfers between devices, shifted(): return lax.ppermute(block, axis, route)  15.5 us
    ppermute x6, starting transfers between devices, shifted(): return lax.ppermute(block, axis, route)  15.1 us
    squeeze x24, local copies, waits for them, and re-layouts, window_gradient(): lax.scan(add_intensity, jnp.zeros((WIN, WIN), jnp.float32), (mode_pairs,...  10.4 us
    another operation x16, other arithmetic  10.3 us
    ppermute x2, starting transfers between devices, with_halo(): lax.ppermute(lax.slice_in_dim(block, 0, width, axis=dim), axis, backward)  6 us
    dot_general x12, matrix products, fields(): jnp.einsum('fx,kfh->kxh', stacked, rotated, preferred_element_type=jnp.fl...  5.89 us
    ppermute x2, starting transfers between devices, with_halo(): lax.ppermute(lax.slice_in_dim(block, block.shape[dim] - width, None, axis...  5.4 us
  transfers between devices with their start and end apart: 10, of which 5 were waited for; matrix products, arithmetic and copies ran while one was open for 20% of the time, Pallas kernels for 0%

commit v1 on v0

v1 whole, which is shorter than its diff:
```python
import math

import jax
import jax.numpy as jnp
import numpy as np
from jax import lax
from jax.experimental import pallas as pl
from jax.experimental.pallas import tpu as pltpu
from jax.sharding import PartitionSpec as P

TILE = 256
MARGIN = 64
MODES = 64
KERN = 12
HALF = 128
WIN = 384
COARSE = 128
STEP = WIN // COARSE

steepness = 4.0
threshold = 0.4
step_rate = 16.0
area = float(WIN * WIN)

VMEM = pltpu.VMEM
BF16 = jnp.bfloat16
F32 = jnp.float32


def tables():
    freq = np.arange(MODES) - MODES // 2
    angle = (2.0 * math.pi / WIN) * np.mod(freq[:, None] * np.arange(WIN)[None], WIN)
    cos, sin = np.cos(angle), np.sin(angle)
    stacked = np.concatenate([cos, sin], 0)
    forward = stacked.T
    core = slice(MARGIN, MARGIN + TILE)
    c_core, s_core = cos[:, core], sin[:, core]
    c_low, s_low = cos[:, ::STEP], sin[:, ::STEP]
    reach = HALF + MARGIN
    place_a = np.zeros((TILE, 2 * MODES))
    place_a[TILE - reach :] = forward[:reach]
    place_b = np.zeros((TILE, 2 * MODES))
    place_b[:reach] = forward[reach:]
    offset = np.arange(MARGIN, MARGIN + TILE)[:, None] - STEP * np.arange(COARSE)[None]
    orders = np.arange(1, 2 * MODES // 2)
    interp = 1.0 + 2.0 * np.cos((2.0 * math.pi / WIN) * orders[:, None, None] * offset[None]).sum(0)
    interp = (interp + np.cos((2.0 * math.pi / WIN) * MODES * offset)) / COARSE
    high = interp.astype(jnp.bfloat16).astype(np.float64)
    table = dict(
        own=forward[core],
        rim=np.concatenate([forward[MARGIN + TILE :], forward[:MARGIN]], 0),
        q_own=stacked[:, core],
        q_rim=np.concatenate([stacked[:, :MARGIN], stacked[:, MARGIN + TILE :]], 1),
        spread=np.block([[c_low, s_low], [-s_low, c_low]]),
        q_low=np.concatenate([c_low.T, s_low.T], 1),
        interp=np.concatenate([high, interp - high], 1),
        interp_t=np.concatenate([high.T, (interp - high).T], 0),
        interp_h=high,
        interp_ht=high.T,
        gather=np.block(
            [[c_low.T, -s_low.T, -s_low.T, -c_low.T], [s_low.T, c_low.T, c_low.T, -s_low.T]]
        ),
        q_back=np.concatenate([c_low, s_low], 1),
        inverse=np.block([[c_core, s_core], [-s_core, c_core]]),
        q_inv=np.concatenate([c_core.T, -s_core.T], 1),
        place=np.concatenate([place_a, place_b], 1),
        q_place=np.concatenate([place_a.T, place_b.T], 0),
        inv_left=np.block([[c_core[:, HALF:], s_core[:, HALF:]], [-s_core[:, HALF:], c_core[:, HALF:]]]),
        inv_right=np.block([[c_core[:, :HALF], s_core[:, :HALF]], [-s_core[:, :HALF], c_core[:, :HALF]]]),
    )
    return {name: value.astype(jnp.bfloat16) for name, value in table.items()}


def dot(left, right):
    return jnp.dot(left, right, preferred_element_type=F32)


def swap_halves(value):
    return pltpu.roll(value, MODES, axis=1)


def low_lanes(shape):
    return lax.broadcasted_iota(jnp.int32, shape, 1) < MODES


def modes_of(blocks):
    top, bottom = blocks[:MODES], swap_halves(blocks[MODES:])
    return jnp.where(low_lanes(top.shape), top - bottom, -(top + bottom)) / area


def imaging_modes(spec, goal, weight, modes_ref, weight_ref, field_ref, grad_ref, t):
    swapped = swap_halves(spec)
    low = low_lanes(spec.shape)
    spec_a = jnp.where(low, spec, swapped)
    spec_b = jnp.where(low, -swapped, spec)
    filtered = []
    for k in range(KERN):
        resp = modes_ref[k]
        filtered.append((resp * spec_a + swap_halves(resp) * spec_b).astype(BF16))
    partial = dot(jnp.concatenate(filtered, 0), t["spread"][...]).astype(BF16)
    level = jnp.zeros((COARSE, COARSE), F32)
    for k in range(KERN):
        part = partial[k * MODES : (k + 1) * MODES]
        real, imag = part[:, :COARSE], part[:, COARSE:]
        rotated = jnp.concatenate([part, jnp.concatenate([-imag, real], 1)], 0)
        field = dot(t["q_low"][...], rotated)
        field_ref[k] = field
        a_real, a_imag = field[:, :COARSE], field[:, COARSE:]
        level = level + weight_ref[k] * (a_real * a_real + a_imag * a_imag)
    level = level.astype(BF16)
    half = dot(t["interp"][...], jnp.concatenate([level, level], 0)).astype(BF16)
    core = dot(jnp.concatenate([half, half], 1), t["interp_t"][...])
    printed = jax.nn.sigmoid(steepness * (core - threshold))
    core_grad = 2.0 * (printed - goal.astype(F32)) * printed * (1.0 - printed) * steepness
    if weight is not None:
        core_grad = jnp.where(weight, core_grad, 0.0)
    low_grad = dot(t["interp_ht"][...], core_grad.astype(BF16)).astype(BF16)
    low_grad = dot(low_grad, t["interp_h"][...])
    both = jnp.concatenate([low_grad, low_grad], 1)
    for k in range(KERN):
        scaled = field_ref[k] * both * (2.0 * weight_ref[k])
        grad_ref[k * COARSE : (k + 1) * COARSE, :] = scaled.astype(BF16)
    gathered = dot(grad_ref[...], t["gather"][...]).astype(BF16)
    direct = jnp.zeros((MODES, 2 * MODES), F32)
    crossed = jnp.zeros((MODES, 2 * MODES), F32)
    for k in range(KERN):
        rows = gathered[k * COARSE : (k + 1) * COARSE]
        back = dot(t["q_back"][...], jnp.concatenate([rows[:, :COARSE], rows[:, COARSE:]], 0))
        resp = modes_ref[k]
        direct = direct + resp * back
        crossed = crossed + swap_halves(resp) * back
    return jnp.where(low, direct + swap_halves(direct), crossed - swap_halves(crossed)).astype(BF16)


def edges_kernel(mask_ref, out_ref):
    wire = jax.nn.sigmoid(mask_ref[...])
    out_ref[...] = jnp.concatenate([wire[:, :MARGIN], wire[:, TILE - MARGIN :]], 1).astype(BF16)


def strip_kernel(cols, mask_ref, left_ref, right_ref, own_ref, rim_ref, u_ref, top_ref, bottom_ref):
    col = lax.axis_index("col")
    wire = jax.nn.sigmoid(mask_ref[...]).astype(BF16)
    low = low_lanes((TILE, 2 * MARGIN))
    keep = jnp.logical_or(
        jnp.logical_and(low, col < cols - 1), jnp.logical_and(jnp.logical_not(low), col > 0)
    )
    rim = jnp.where(low, right_ref[...].astype(F32), left_ref[...].astype(F32))
    rim = jnp.where(keep, rim, 0.0).astype(BF16)
    half_spec = (dot(wire, own_ref[...]) + dot(rim, rim_ref[...])).astype(BF16)
    u_ref[...] = half_spec
    top_ref[...] = half_spec[:MARGIN]
    bottom_ref[...] = half_spec[TILE - MARGIN :]


FIRST_TABLES = (
    "q_own", "q_rim", "spread", "q_low", "interp", "interp_t", "interp_h", "interp_ht",
    "gather", "q_back", "inverse", "q_inv", "place", "q_place",
)


def first_kernel(rows, *refs):
    mask_ref, u_ref, above_ref, below_ref, goal_ref, modes_ref, weight_ref = refs[:7]
    t = dict(zip(FIRST_TABLES, refs[7 : 7 + len(FIRST_TABLES)]))
    first_ref, aa_ref, ab_ref, ba_ref, bb_ref, field_ref, grad_ref = refs[7 + len(FIRST_TABLES) :]
    row = lax.axis_index("row")
    above = jnp.where(row > 0, above_ref[...].astype(F32), 0.0)
    below = jnp.where(row < rows - 1, below_ref[...].astype(F32), 0.0)
    rim = jnp.concatenate([above, below], 0).astype(BF16)
    spec = modes_of(dot(t["q_own"][...], u_ref[...]) + dot(t["q_rim"][...], rim))
    combined = imaging_modes(
        spec, goal_ref[...], None, modes_ref, weight_ref, field_ref, grad_ref, t
    )
    back = dot(combined, t["inverse"][...]).astype(BF16)
    mask_grad = dot(t["q_inv"][...], jnp.concatenate([back[:, :TILE], back[:, TILE:]], 0)) / area
    mask = mask_ref[...]
    soft = jax.nn.sigmoid(mask)
    first = mask - step_rate * (mask_grad * soft * (1.0 - soft))
    first_ref[...] = first
    wire = jax.nn.sigmoid(first).astype(BF16)
    half = dot(wire, t["place"][...])
    half_hi = half.astype(BF16)
    half_lo = (half - half_hi.astype(F32)).astype(BF16)
    blocks = dot(t["q_place"][...], half_hi) + dot(t["q_place"][...], half_lo)
    aa_ref[...] = modes_of(blocks[:HALF, :HALF])
    ab_ref[...] = modes_of(blocks[:HALF, HALF:])
    ba_ref[...] = modes_of(blocks[HALF:, :HALF])
    bb_ref[...] = modes_of(blocks[HALF:, HALF:])


HEAL_TABLES = (
    "spread", "q_low", "interp", "interp_t", "interp_h", "interp_ht", "gather", "q_back",
)


def heal_kernel(rows, cols, *refs):
    own_ref, right_ref, below_ref, corner_ref = refs[:4]
    goal_ref, goal_right_ref, goal_below_ref, modes_ref, weight_ref = refs[4:9]
    t = dict(zip(HEAL_TABLES, refs[9 : 9 + len(HEAL_TABLES)]))
    out_ref, field_ref, grad_ref = refs[9 + len(HEAL_TABLES) :]
    inner_row = lax.axis_index("row") < rows - 1
    inner_col = lax.axis_index("col") < cols - 1
    spec = own_ref[...]
    spec = spec + jnp.where(inner_col, right_ref[...], 0.0)
    spec = spec + jnp.where(inner_row, below_ref[...], 0.0)
    spec = spec + jnp.where(jnp.logical_and(inner_row, inner_col), corner_ref[...], 0.0)
    upper = jnp.concatenate([goal_ref[HALF:, HALF:], goal_right_ref[HALF:, :]], 1)
    goal = jnp.concatenate([upper, goal_below_ref[...]], 0)
    shape = (TILE, TILE)
    weight = jnp.logical_and(
        jnp.logical_or(lax.broadcasted_iota(jnp.int32, shape, 0) < HALF, inner_row),
        jnp.logical_or(lax.broadcasted_iota(jnp.int32, shape, 1) < HALF, inner_col),
    )
    out_ref[...] = imaging_modes(
        spec, goal, weight, modes_ref, weight_ref, field_ref, grad_ref, t
    )


def final_kernel(first_ref, own_ref, left_ref, up_ref, corner_ref, inv_left_ref, inv_right_ref, q_inv_ref, out_ref):
    has_row = lax.axis_index("row") > 0
    has_col = lax.axis_index("col") > 0

    def kept(ref, flag):
        return jnp.where(flag, ref[...].astype(F32), 0.0).astype(BF16)

    left = jnp.concatenate(
        [kept(left_ref, has_col), kept(corner_ref, jnp.logical_and(has_row, has_col))], 0
    )
    right = jnp.concatenate([own_ref[...], kept(up_ref, has_row)], 0)
    left = dot(left, inv_left_ref[...]).astype(BF16)
    right = dot(right, inv_right_ref[...]).astype(BF16)

    def quarter(rows):
        real = jnp.concatenate([left[rows, :HALF], right[rows, :HALF]], 1)
        imag = jnp.concatenate([left[rows, HALF:], right[rows, HALF:]], 1)
        return jnp.concatenate([real, imag], 0)

    lower = dot(q_inv_ref[:HALF, :], quarter(slice(0, MODES)))
    upper = dot(q_inv_ref[HALF:, :], quarter(slice(MODES, 2 * MODES)))
    grad = jnp.concatenate([upper, lower], 0) / area
    first = first_ref[...]
    soft = jax.nn.sigmoid(first)
    out_ref[...] = first - step_rate * (grad * soft * (1.0 - soft))


def vmem(count):
    return [pl.BlockSpec(memory_space=VMEM)] * count


SMEM_SPEC = pl.BlockSpec(memory_space=pltpu.SMEM)
FIELD_SCRATCH = [VMEM((KERN, COARSE, 2 * COARSE), F32), VMEM((KERN * COARSE, 2 * COARSE), BF16)]


def shape_of(rows, cols, dtype):
    return jax.ShapeDtypeStruct((rows, cols), dtype)


def per_device(rows, cols, mask_param, target, kernel_modes, kernel_weight):
    table = {name: jnp.asarray(value) for name, value in tables().items()}

    def move(value, down, right):
        pairs = [
            (r * cols + c, ((r + down) % rows) * cols + (c + right) % cols)
            for r in range(rows)
            for c in range(cols)
        ]
        return lax.ppermute(value, ("row", "col"), pairs)

    edges = pl.pallas_call(
        edges_kernel, out_shape=shape_of(TILE, 2 * MARGIN, BF16), in_specs=vmem(1),
        out_specs=vmem(1)[0], name="edges",
    )(mask_param)
    from_left = move(edges, 0, 1)
    from_right = move(edges, 0, -1)
    goal_right = move(target[:, :HALF], 0, -1)
    half_spec, top, bottom = pl.pallas_call(
        lambda *refs: strip_kernel(cols, *refs),
        out_shape=(
            shape_of(TILE, 2 * MODES, BF16), shape_of(MARGIN, 2 * MODES, BF16),
            shape_of(MARGIN, 2 * MODES, BF16),
        ),
        in_specs=vmem(5), out_specs=tuple(vmem(3)), name="strip",
    )(mask_param, from_left, from_right, table["own"], table["rim"])
    above = move(bottom, 1, 0)
    below = move(top, -1, 0)
    goal_below = move(jnp.concatenate([target[:HALF, HALF:], goal_right[:HALF]], 1), -1, 0)
    modes_shape = shape_of(MODES, 2 * MODES, F32)
    first, own, to_left, to_up, to_corner = pl.pallas_call(
        lambda *refs: first_kernel(rows, *refs),
        out_shape=(shape_of(TILE, TILE, F32),) + (modes_shape,) * 4,
        in_specs=vmem(6) + [SMEM_SPEC] + vmem(len(FIRST_TABLES)), out_specs=tuple(vmem(5)),
        scratch_shapes=FIELD_SCRATCH, name="first",
    )(
        mask_param, half_spec, above, below, target, kernel_modes, kernel_weight,
        *[table[name] for name in FIRST_TABLES],
    )
    spec_right = move(to_left, 0, -1)
    spec_below = move(to_up, -1, 0)
    spec_corner = move(to_corner, -1, -1)
    combined = pl.pallas_call(
        lambda *refs: heal_kernel(rows, cols, *refs),
        out_shape=shape_of(MODES, 2 * MODES, BF16),
        in_specs=vmem(8) + [SMEM_SPEC] + vmem(len(HEAL_TABLES)), out_specs=vmem(1)[0],
        scratch_shapes=FIELD_SCRATCH, name="heal",
    )(
        own, spec_right, spec_below, spec_corner, target, goal_right, goal_below,
        kernel_modes, kernel_weight, *[table[name] for name in HEAL_TABLES],
    )
    mode_left = move(combined, 0, 1)
    mode_up = move(combined, 1, 0)
    mode_corner = move(combined, 1, 1)
    return pl.pallas_call(
        final_kernel, out_shape=shape_of(TILE, TILE, F32), in_specs=vmem(8),
        out_specs=vmem(1)[0], name="final",
    )(
        first, combined, mode_left, mode_up, mode_corner,
        table["inv_left"], table["inv_right"], table["q_inv"],
    )


def solution(mesh):
    rows, cols = mesh.shape["row"], mesh.shape["col"]
    tile = P(("grp", "row"), "col")
    return jax.shard_map(
        lambda *args: per_device(rows, cols, *args), mesh=mesh,
        in_specs=(tile, tile, P(), P()), out_specs=tile, check_vma=False,
    )
```

time: 139 us -> 48.6 us (0.35)
  the two profiles are of different devices: /device:TPU:10 before, /device:TPU:0 now
where the time goes in v1:
time: 48.6 us; the launch traced here: 48.3 us
  starting transfers between devices  16.9 us (35%)
  Pallas kernels  14.8 us (30%)
  waiting for transfers between devices  11.2 us (23%)
  local copies, waits for them, and re-layouts  5.28 us (11%)
    ppermute x12, starting transfers between devices, move(): return lax.ppermute(value, ('row', 'col'), pairs)  16.9 us
    ppermute x12, waiting for transfers between devices, move(): return lax.ppermute(value, ('row', 'col'), pairs)  11.2 us
    pallas_call x1, Pallas kernels, per_device(): pl.pallas_call(lambda *refs: first_kernel(rows, *refs), out_shape=(shape_...  5.18 us
    pallas_call x1, Pallas kernels, per_device(): pl.pallas_call(lambda *refs: heal_kernel(rows, cols, *refs), out_shape=sh...  4.01 us
    unnamed x24, local copies, waits for them, and re-layouts  3.67 us
    pallas_call x1, Pallas kernels, per_device(): pl.pallas_call(final_kernel, out_shape=shape_of(TILE, TILE, F32), in_spec...  2.1 us
    pallas_call x1, Pallas kernels, per_device(): pl.pallas_call(lambda *refs: strip_kernel(cols, *refs), out_shape=(shape_...  1.87 us
    pallas_call x1, Pallas kernels, per_device(): pl.pallas_call(edges_kernel, out_shape=shape_of(TILE, 2 * MARGIN, BF16),...  1.62 us
  transfers between devices with their start and end apart: 12, of which 6 were waited for; matrix products, arithmetic and copies ran while one was open for 2% of the time, Pallas kernels for 18%

profile of v1, /device:TPU:0, one launch (start us, length us, event | category | flops | bytes accessed | tf_op | source)
XLA Modules:
  0.0 48.3 jit_solution(4633423641406520174)
XLA Ops:
  0.0 0.8 %slice.9 = bf16[256,128]{1,0:T(8,128)(2,1)S(1)} slice(bf16[256,256]{1,0:T(8,128)(2,1)} %refs_4_.4), slice={[0:256], [0:128]} | slice | bytes 131072 | tf_op jit(solution)/shard_map/slice | solution.py:274
  0.8 2.4 %collective-permute-start.7 = (bf16[256,128]{1,0:T(8,128)(2,1)S(1)}, bf16[256,128]{1,0:T(8,128)(2,1)S(1)}, u32[]{:S(2)}, u32[]{:S(2)}) collective-permute-start(bf16[256,128]{1,0:T(8,128)(2,1)S(1)} %slice.9), channel_id=1, source_target_pairs={{0,3},{1,0},{2,1},{3,2},{4,7},{5,4},{6,5},{7,6},{8,11},{9,8},{10,9... | collective-permute-start | bytes 196616 | tf_op jit(solution)/shard_map/ppermute | solution.py:266
  3.3 1.6 %edges.1 = bf16[256,128]{1,0:T(8,128)(2,1)} custom-call(f32[256,256]{1,0:T(8,128)} %refs_0_.3), custom_call_target="tpu_custom_call" | custom-call | tf_op jit(solution)/shard_map/edges/pallas_call | solution.py:268
  4.9 0.0 collective-permute-start
  4.9 1.7 %collective-permute-start.1 = (bf16[256,128]{1,0:T(8,128)(2,1)}, bf16[256,128]{1,0:T(8,128)(2,1)S(1)}, u32[]{:S(2)}, u32[]{:S(2)}) collective-permute-start(bf16[256,128]{1,0:T(8,128)(2,1)} %edges.1), channel_id=1, source_target_pairs={{0,3},{1,0},{2,1},{3,2},{4,7},{5,4},{6,5},{7,6},{8,11},{9,8},{10,9... | collective-permute-start | bytes 196616 | tf_op jit(solution)/shard_map/ppermute | solution.py:266
  6.6 0.8 %slice.10 = bf16[128,128]{1,0:T(8,128)(2,1)S(1)} slice(bf16[256,256]{1,0:T(8,128)(2,1)} %refs_4_.4), slice={[0:128], [128:256]} | slice | bytes 65536 | tf_op jit(solution)/shard_map/slice | solution.py:285
  7.4 0.0 collective-permute-done.7.refs_5_
  7.4 0.0 copy-start
  7.4 0.6 %copy-done = bf16[256,128]{1,0:T(8,128)(2,1)} copy-done((bf16[256,128]{1,0:T(8,128)(2,1)}, bf16[256,128]{1,0:T(8,128)(2,1)S(1)}, u32[]{:S(2)}) %copy-start) | copy-done | bytes 65560
  8.0 3.6 %collective-permute-start.8 = (bf16[128,256]{1,0:T(8,128)(2,1)S(1)}, bf16[128,256]{1,0:T(8,128)(2,1)S(1)}, u32[]{:S(2)}, u32[]{:S(2)}) collective-permute-start(bf16[128,256]{1,0:T(8,128)(2,1)S(1)} %pad_maximum_fusion), channel_id=1, source_target_pairs={{0,12},{1,13},{2,14},{3,15},{4,0},{5,1},{6,2},{7,3},{8,4},{9,5},{1... | collective-permute-start | bytes 196616 | tf_op jit(solution)/shard_map/ppermute | solution.py:266
  11.6 0.0 collective-permute-done.refs_1_
  11.6 0.0 copy-start.1
  11.6 0.0 collective-permute-done.1.refs_2_
  11.6 0.6 %copy-done.1 = bf16[256,128]{1,0:T(8,128)(2,1)} copy-done((bf16[256,128]{1,0:T(8,128)(2,1)}, bf16[256,128]{1,0:T(8,128)(2,1)S(1)}, u32[]{:S(2)}) %copy-start.1) | copy-done | bytes 65560
  12.2 0.0 copy-start.2
  12.2 0.6 %copy-done.2 = bf16[256,128]{1,0:T(8,128)(2,1)} copy-done((bf16[256,128]{1,0:T(8,128)(2,1)}, bf16[256,128]{1,0:T(8,128)(2,1)S(1)}, u32[]{:S(2)}) %copy-start.2) | copy-done | bytes 65560
  12.9 1.9 %strip.1 = (bf16[256,128]{1,0:T(8,128)(2,1)}, bf16[64,128]{1,0:T(8,128)(2,1)}, bf16[64,128]{1,0:T(8,128)(2,1)}) custom-call(f32[256,256]{1,0:T(8,128)} %refs_0_.3, bf16[256,128]{1,0:T(8,128)(2,1)} %copy-done.1, bf16[256,128]{1,0:T(8,128)(2,1)} %copy-done.2, bf16[256,128]{1,0:T(8,128)(2,1)} %constant.36.clone.refs_3_, bf16[128,128]{1,0:T(8,128)(2,1)} %constant.37.clone.refs_4_), custom_call_target="tpu_custom_call" | custom-call | tf_op jit(solution)/shard_map/strip/pallas_call | solution.py:275
  14.7 0.0 collective-permute-start.2
  14.7 3.8 %collective-permute-start.3 = (bf16[64,128]{1,0:T(8,128)(2,1)}, bf16[64,128]{1,0:T(8,128)(2,1)S(1)}, u32[]{:S(2)}, u32[]{:S(2)}) collective-permute-start(bf16[64,128]{1,0:T(8,128)(2,1)} %get-tuple-element.15), channel_id=1, source_target_pairs={{0,12},{1,13},{2,14},{3,15},{4,0},{5,1},{6,2},{7,3},{8,4},{9,5},{1... | collective-permute-start | bytes 49160 | tf_op jit(solution)/shard_map/ppermute | solution.py:266
  18.6 1.9 %collective-permute-done.2.refs_2_ = bf16[64,128]{1,0:T(8,128)(2,1)S(1)} collective-permute-done((bf16[64,128]{1,0:T(8,128)(2,1)}, bf16[64,128]{1,0:T(8,128)(2,1)S(1)}, u32[]{:S(2)}, u32[]{:S(2)}) %collective-permute-start.2) | collective-permute-done | bytes 16416 | tf_op jit(solution)/shard_map/ppermute | solution.py:266
  20.5 0.0 copy-start.7
  20.5 0.0 collective-permute-done.3.refs_3_
  20.5 0.0 copy-start.8
  20.5 0.6 %copy-done.7 = bf16[64,128]{1,0:T(8,128)(2,1)} copy-done((bf16[64,128]{1,0:T(8,128)(2,1)}, bf16[64,128]{1,0:T(8,128)(2,1)S(1)}, u32[]{:S(2)}) %copy-start.7) | copy-done | bytes 16408
  21.1 0.0 copy-done.8
  21.1 5.2 %first.1 = (f32[256,256]{1,0:T(8,128)}, f32[64,128]{1,0:T(8,128)}, f32[64,128]{1,0:T(8,128)}, f32[64,128]{1,0:T(8,128)}, f32[64,128]{1,0:T(8,128)}) custom-call(f32[256,256]{1,0:T(8,128)} %refs_0_.3, bf16[256,128]{1,0:T(8,128)(2,1)} %get-tuple-element.13.refs_1_, bf16[64,128]{1,0:T(8,128)(2,1)} %copy-done.7, bf16[64,128]{1,0:T(8,128)(2,1)} %copy-done.8, ...), custom_call_target="tpu_custom_call" | custom-call | tf_op jit(solution)/shard_map/first/pallas_call | solution.py:287
  26.3 0.0 collective-permute-start.4
  26.3 3.9 %collective-permute-start.5 = (f32[64,128]{1,0:T(8,128)}, f32[64,128]{1,0:T(8,128)S(1)}, u32[]{:S(2)}, u32[]{:S(2)}) collective-permute-start(f32[64,128]{1,0:T(8,128)} %get-tuple-element.19), channel_id=1, source_target_pairs={{0,12},{1,13},{2,14},{3,15},{4,0},{5,1},{6,2},{7,3},{8,4},{9,5},{1... | collective-permute-start | bytes 98312 | tf_op jit(solution)/shard_map/ppermute | solution.py:266
  30.2 0.1 collective-permute-start.6
  30.2 0.0 collective-permute-done.4.refs_1_
  30.3 0.0 copy-start.4
  30.3 1.9 %collective-permute-done.5.refs_2_ = f32[64,128]{1,0:T(8,128)S(1)} collective-permute-done((f32[64,128]{1,0:T(8,128)}, f32[64,128]{1,0:T(8,128)S(1)}, u32[]{:S(2)}, u32[]{:S(2)}) %collective-permute-start.5) | collective-permute-done | bytes 32800 | tf_op jit(solution)/shard_map/ppermute | solution.py:266
  32.1 0.0 copy-start.5
  32.1 1.6 %collective-permute-done.6.refs_3_ = f32[64,128]{1,0:T(8,128)S(1)} collective-permute-done((f32[64,128]{1,0:T(8,128)}, f32[64,128]{1,0:T(8,128)S(1)}, u32[]{:S(2)}, u32[]{:S(2)}) %collective-permute-start.6) | collective-permute-done | bytes 32800 | tf_op jit(solution)/shard_map/ppermute | solution.py:266
  33.7 0.0 copy-start.6
  33.7 0.0 collective-permute-done.8.refs_6_
  33.7 0.0 copy-start.3
  33.7 0.0 copy-done.4
  33.8 0.0 copy-done.5
  33.8 0.6 %copy-done.6 = f32[64,128]{1,0:T(8,128)} copy-done((f32[64,128]{1,0:T(8,128)}, f32[64,128]{1,0:T(8,128)S(1)}, u32[]{:S(2)}) %copy-start.6) | copy-done | bytes 32792
  34.3 0.0 copy-done.3
  34.4 4.0 %heal.1.own_ref = bf16[64,128]{1,0:T(8,128)(2,1)} custom-call(f32[64,128]{1,0:T(8,128)} %get-tuple-element.17.refs_0_, f32[64,128]{1,0:T(8,128)} %copy-done.4, f32[64,128]{1,0:T(8,128)} %copy-done.5, f32[64,128]{1,0:T(8,128)} %copy-done.6, bf16[256,256]{1,0:T(8,128)(2,1)} %refs_4_.4, bf16[256,128]{1,0:T(8,128)(2,1)} %copy-done, bf16[128,256]{1,0:T(8,128)(2,1)} %copy-done.3, ...), custom_call_target="tpu_custom_call" | custom-call | tf_op jit(solution)/shard_map/heal/pallas_call | solution.py:299
  38.4 1.1 %collective-permute-start.9 = (bf16[64,128]{1,0:T(8,128)(2,1)}, bf16[64,128]{1,0:T(8,128)(2,1)S(1)}, u32[]{:S(2)}, u32[]{:S(2)}) collective-permute-start(bf16[64,128]{1,0:T(8,128)(2,1)} %heal.1.own_ref), channel_id=1, source_target_pairs={{0,1},{1,2},{2,3},{3,0},{4,5},{5,6},{6,7},{7,4},{8,9},{9,10},{10,1... | collective-permute-start | bytes 49160 | tf_op jit(solution)/shard_map/ppermute | solution.py:266
  39.5 0.0 collective-permute-start.10
  39.5 0.3 collective-permute-start.11
  39.7 2.0 %collective-permute-done.9.left_ref = bf16[64,128]{1,0:T(8,128)(2,1)S(1)} collective-permute-done((bf16[64,128]{1,0:T(8,128)(2,1)}, bf16[64,128]{1,0:T(8,128)(2,1)S(1)}, u32[]{:S(2)}, u32[]{:S(2)}) %collective-permute-start.9) | collective-permute-done | bytes 16416 | tf_op jit(solution)/shard_map/ppermute | solution.py:266
  41.8 0.0 copy-start.9
  41.8 3.4 %collective-permute-done.10.up_ref = bf16[64,128]{1,0:T(8,128)(2,1)S(1)} collective-permute-done((bf16[64,128]{1,0:T(8,128)(2,1)}, bf16[64,128]{1,0:T(8,128)(2,1)S(1)}, u32[]{:S(2)}, u32[]{:S(2)}) %collective-permute-start.10) | collective-permute-done | bytes 16416 | tf_op jit(solution)/shard_map/ppermute | solution.py:266
  45.2 0.0 copy-start.10
  45.2 0.4 collective-permute-done.11.corner_ref
  45.6 0.0 copy-start.11
  45.6 0.0 copy-done.9
  45.6 0.2 copy-done.10
  45.8 0.3 copy-done.11
  46.2 2.1 %final.1 = f32[256,256]{1,0:T(8,128)} custom-call(f32[256,256]{1,0:T(8,128)} %get-tuple-element.16.first_ref, bf16[64,128]{1,0:T(8,128)(2,1)} %heal.1.own_ref, bf16[64,128]{1,0:T(8,128)(2,1)} %copy-done.9, bf16[64,128]{1,0:T(8,128)(2,1)} %copy-done.10, bf16[64,128]{1,0:T(8,128)(2,1)} %copy-done.11, bf16[128,256]{1,0:T(8,128)(2,1)} %constant.52.clone.inv_left_ref, ...), custom_call_target="tpu_custom_call" | custom-call | tf_op jit(solution)/shard_map/final/pallas_call | solution.py:311
  (2 shorter events, 0.0 us)
Async XLA Ops:
  0.8 6.5 %collective-permute-start.7 = (bf16[256,128]{1,0:T(8,128)(2,1)S(1)}, bf16[256,128]{1,0:T(8,128)(2,1)S(1)}, u32[]{:S(2)}, u32[]{:S(2)}) collective-permute-start(bf16[256,128]{1,0:T(8,128)(2,1)S(1)} %slice.9), channel_id=1, source_target_pairs={{0,3},{1,0},{2,1},{3,2},{4,7},{5,4},{6,5},{7,6},{8,11},{9,8},{10,9... | collective-permute-start | bytes 196616 | tf_op jit(solution)/shard_map/ppermute | solution.py:266
  4.9 6.7 %collective-permute-start = (bf16[256,128]{1,0:T(8,128)(2,1)}, bf16[256,128]{1,0:T(8,128)(2,1)S(1)}, u32[]{:S(2)}, u32[]{:S(2)}) collective-permute-start(bf16[256,128]{1,0:T(8,128)(2,1)} %edges.1), channel_id=1, source_target_pairs={{0,1},{1,2},{2,3},{3,0},{4,5},{5,6},{6,7},{7,4},{8,9},{9,10},{10,1... | collective-permute-start | bytes 196616 | tf_op jit(solution)/shard_map/ppermute | solution.py:266
  4.9 6.7 %collective-permute-start.1 = (bf16[256,128]{1,0:T(8,128)(2,1)}, bf16[256,128]{1,0:T(8,128)(2,1)S(1)}, u32[]{:S(2)}, u32[]{:S(2)}) collective-permute-start(bf16[256,128]{1,0:T(8,128)(2,1)} %edges.1), channel_id=1, source_target_pairs={{0,3},{1,0},{2,1},{3,2},{4,7},{5,4},{6,5},{7,6},{8,11},{9,8},{10,9... | collective-permute-start | bytes 196616 | tf_op jit(solution)/shard_map/ppermute | solution.py:266
  7.4 0.6 %copy-start = (bf16[256,128]{1,0:T(8,128)(2,1)}, bf16[256,128]{1,0:T(8,128)(2,1)S(1)}, u32[]{:S(2)}) copy-start(bf16[256,128]{1,0:T(8,128)(2,1)S(1)} %collective-permute-done.7.refs_5_) | copy-start | bytes 196612
  8.0 25.7 %collective-permute-start.8 = (bf16[128,256]{1,0:T(8,128)(2,1)S(1)}, bf16[128,256]{1,0:T(8,128)(2,1)S(1)}, u32[]{:S(2)}, u32[]{:S(2)}) collective-permute-start(bf16[128,256]{1,0:T(8,128)(2,1)S(1)} %pad_maximum_fusion), channel_id=1, source_target_pairs={{0,12},{1,13},{2,14},{3,15},{4,0},{5,1},{6,2},{7,3},{8,4},{9,5},{1... | collective-permute-start | bytes 196616 | tf_op jit(solution)/shard_map/ppermute | solution.py:266
  11.6 0.6 %copy-start.1 = (bf16[256,128]{1,0:T(8,128)(2,1)}, bf16[256,128]{1,0:T(8,128)(2,1)S(1)}, u32[]{:S(2)}) copy-start(bf16[256,128]{1,0:T(8,128)(2,1)S(1)} %collective-permute-done.refs_1_) | copy-start | bytes 196612
  12.2 0.6 %copy-start.2 = (bf16[256,128]{1,0:T(8,128)(2,1)}, bf16[256,128]{1,0:T(8,128)(2,1)S(1)}, u32[]{:S(2)}) copy-start(bf16[256,128]{1,0:T(8,128)(2,1)S(1)} %collective-permute-done.1.refs_2_) | copy-start | bytes 196612
  14.7 5.7 %collective-permute-start.2 = (bf16[64,128]{1,0:T(8,128)(2,1)}, bf16[64,128]{1,0:T(8,128)(2,1)S(1)}, u32[]{:S(2)}, u32[]{:S(2)}) collective-permute-start(bf16[64,128]{1,0:T(8,128)(2,1)} %get-tuple-element.14), channel_id=1, source_target_pairs={{0,4},{1,5},{2,6},{3,7},{4,8},{5,9},{6,10},{7,11},{8,12},{9,13},{1... | collective-permute-start | bytes 49160 | tf_op jit(solution)/shard_map/ppermute | solution.py:266
  14.7 5.7 %collective-permute-start.3 = (bf16[64,128]{1,0:T(8,128)(2,1)}, bf16[64,128]{1,0:T(8,128)(2,1)S(1)}, u32[]{:S(2)}, u32[]{:S(2)}) collective-permute-start(bf16[64,128]{1,0:T(8,128)(2,1)} %get-tuple-element.15), channel_id=1, source_target_pairs={{0,12},{1,13},{2,14},{3,15},{4,0},{5,1},{6,2},{7,3},{8,4},{9,5},{1... | collective-permute-start | bytes 49160 | tf_op jit(solution)/shard_map/ppermute | solution.py:266
  20.5 0.6 %copy-start.7 = (bf16[64,128]{1,0:T(8,128)(2,1)}, bf16[64,128]{1,0:T(8,128)(2,1)S(1)}, u32[]{:S(2)}) copy-start(bf16[64,128]{1,0:T(8,128)(2,1)S(1)} %collective-permute-done.2.refs_2_) | copy-start | bytes 49156
  20.5 0.6 %copy-start.8 = (bf16[64,128]{1,0:T(8,128)(2,1)}, bf16[64,128]{1,0:T(8,128)(2,1)S(1)}, u32[]{:S(2)}) copy-start(bf16[64,128]{1,0:T(8,128)(2,1)S(1)} %collective-permute-done.3.refs_3_) | copy-start | bytes 49156
  26.3 4.0 %collective-permute-start.4 = (f32[64,128]{1,0:T(8,128)}, f32[64,128]{1,0:T(8,128)S(1)}, u32[]{:S(2)}, u32[]{:S(2)}) collective-permute-start(f32[64,128]{1,0:T(8,128)} %get-tuple-element.18), channel_id=1, source_target_pairs={{0,3},{1,0},{2,1},{3,2},{4,7},{5,4},{6,5},{7,6},{8,11},{9,8},{10,9... | collective-permute-start | bytes 98312 | tf_op jit(solution)/shard_map/ppermute | solution.py:266
  26.3 5.8 %collective-permute-start.5 = (f32[64,128]{1,0:T(8,128)}, f32[64,128]{1,0:T(8,128)S(1)}, u32[]{:S(2)}, u32[]{:S(2)}) collective-permute-start(f32[64,128]{1,0:T(8,128)} %get-tuple-element.19), channel_id=1, source_target_pairs={{0,12},{1,13},{2,14},{3,15},{4,0},{5,1},{6,2},{7,3},{8,4},{9,5},{1... | collective-permute-start | bytes 98312 | tf_op jit(solution)/shard_map/ppermute | solution.py:266
  30.2 3.6 %collective-permute-start.6 = (f32[64,128]{1,0:T(8,128)}, f32[64,128]{1,0:T(8,128)S(1)}, u32[]{:S(2)}, u32[]{:S(2)}) collective-permute-start(f32[64,128]{1,0:T(8,128)} %get-tuple-element.20), channel_id=1, source_target_pairs={{0,15},{1,12},{2,13},{3,14},{4,3},{5,0},{6,1},{7,2},{8,7},{9,4},{1... | collective-permute-start | bytes 98312 | tf_op jit(solution)/shard_map/ppermute | solution.py:266
  30.3 3.5 %copy-start.4 = (f32[64,128]{1,0:T(8,128)}, f32[64,128]{1,0:T(8,128)S(1)}, u32[]{:S(2)}) copy-start(f32[64,128]{1,0:T(8,128)S(1)} %collective-permute-done.4.refs_1_) | copy-start | bytes 98308
  32.1 1.6 %copy-start.5 = (f32[64,128]{1,0:T(8,128)}, f32[64,128]{1,0:T(8,128)S(1)}, u32[]{:S(2)}) copy-start(f32[64,128]{1,0:T(8,128)S(1)} %collective-permute-done.5.refs_2_) | copy-start | bytes 98308
  33.7 0.6 %copy-start.6 = (f32[64,128]{1,0:T(8,128)}, f32[64,128]{1,0:T(8,128)S(1)}, u32[]{:S(2)}) copy-start(f32[64,128]{1,0:T(8,128)S(1)} %collective-permute-done.6.refs_3_) | copy-start | bytes 98308
  33.7 0.6 %copy-start.3 = (bf16[128,256]{1,0:T(8,128)(2,1)}, bf16[128,256]{1,0:T(8,128)(2,1)S(1)}, u32[]{:S(2)}) copy-start(bf16[128,256]{1,0:T(8,128)(2,1)S(1)} %collective-permute-done.8.refs_6_) | copy-start | bytes 196612
  38.4 3.4 %collective-permute-start.9 = (bf16[64,128]{1,0:T(8,128)(2,1)}, bf16[64,128]{1,0:T(8,128)(2,1)S(1)}, u32[]{:S(2)}, u32[]{:S(2)}) collective-permute-start(bf16[64,128]{1,0:T(8,128)(2,1)} %heal.1.own_ref), channel_id=1, source_target_pairs={{0,1},{1,2},{2,3},{3,0},{4,5},{5,6},{6,7},{7,4},{8,9},{9,10},{10,1... | collective-permute-start | bytes 49160 | tf_op jit(solution)/shard_map/ppermute | solution.py:266
  39.5 5.7 %collective-permute-start.10 = (bf16[64,128]{1,0:T(8,128)(2,1)}, bf16[64,128]{1,0:T(8,128)(2,1)S(1)}, u32[]{:S(2)}, u32[]{:S(2)}) collective-permute-start(bf16[64,128]{1,0:T(8,128)(2,1)} %heal.1.own_ref), channel_id=1, source_target_pairs={{0,4},{1,5},{2,6},{3,7},{4,8},{5,9},{6,10},{7,11},{8,12},{9,13},{1... | collective-permute-start | bytes 49160 | tf_op jit(solution)/shard_map/ppermute | solution.py:266
  39.5 6.1 %collective-permute-start.11 = (bf16[64,128]{1,0:T(8,128)(2,1)}, bf16[64,128]{1,0:T(8,128)(2,1)S(1)}, u32[]{:S(2)}, u32[]{:S(2)}) collective-permute-start(bf16[64,128]{1,0:T(8,128)(2,1)} %heal.1.own_ref), channel_id=1, source_target_pairs={{0,5},{1,6},{2,7},{3,4},{4,9},{5,10},{6,11},{7,8},{8,13},{9,14},{1... | collective-permute-start | bytes 49160 | tf_op jit(solution)/shard_map/ppermute | solution.py:266
  41.8 3.8 %copy-start.9 = (bf16[64,128]{1,0:T(8,128)(2,1)}, bf16[64,128]{1,0:T(8,128)(2,1)S(1)}, u32[]{:S(2)}) copy-start(bf16[64,128]{1,0:T(8,128)(2,1)S(1)} %collective-permute-done.9.left_ref) | copy-start | bytes 49156
  45.2 0.6 %copy-start.10 = (bf16[64,128]{1,0:T(8,128)(2,1)}, bf16[64,128]{1,0:T(8,128)(2,1)S(1)}, u32[]{:S(2)}) copy-start(bf16[64,128]{1,0:T(8,128)(2,1)S(1)} %collective-permute-done.10.up_ref) | copy-start | bytes 49156
  45.6 0.6 %copy-start.11 = (bf16[64,128]{1,0:T(8,128)(2,1)}, bf16[64,128]{1,0:T(8,128)(2,1)S(1)}, u32[]{:S(2)}) copy-start(bf16[64,128]{1,0:T(8,128)(2,1)S(1)} %collective-permute-done.11.corner_ref) | copy-start | bytes 49156

commit v2 on v1

v2 whole, which is shorter than its diff:
```python
import math

import jax
import jax.numpy as jnp
import numpy as np
from jax import lax
from jax.experimental import pallas as pl
from jax.experimental.pallas import tpu as pltpu
from jax.sharding import PartitionSpec as P

TILE = 256
MARGIN = 64
MODES = 64
KERN = 12
HALF = 128
WIN = 384
COARSE = 128
STEP = WIN // COARSE

steepness = 4.0
threshold = 0.4
step_rate = 16.0
area = float(WIN * WIN)

VMEM = pltpu.VMEM
BF16 = jnp.bfloat16
F32 = jnp.float32


def tables():
    freq = np.arange(MODES) - MODES // 2
    angle = (2.0 * math.pi / WIN) * np.mod(freq[:, None] * np.arange(WIN)[None], WIN)
    cos, sin = np.cos(angle), np.sin(angle)
    stacked = np.concatenate([cos, sin], 0)
    forward = stacked.T
    core = slice(MARGIN, MARGIN + TILE)
    c_core, s_core = cos[:, core], sin[:, core]
    c_low, s_low = cos[:, ::STEP], sin[:, ::STEP]
    reach = HALF + MARGIN
    place_a = np.zeros((TILE, 2 * MODES))
    place_a[TILE - reach :] = forward[:reach]
    place_b = np.zeros((TILE, 2 * MODES))
    place_b[:reach] = forward[reach:]
    offset = np.arange(MARGIN, MARGIN + TILE)[:, None] - STEP * np.arange(COARSE)[None]
    orders = np.arange(1, 2 * MODES // 2)
    interp = 1.0 + 2.0 * np.cos((2.0 * math.pi / WIN) * orders[:, None, None] * offset[None]).sum(0)
    interp = (interp + np.cos((2.0 * math.pi / WIN) * MODES * offset)) / COARSE
    high = interp.astype(jnp.bfloat16).astype(np.float64)
    pad = np.zeros((COARSE, COARSE))
    table = dict(
        own=(forward[core], np.concatenate([c_core.T, -s_core.T], 1)),
        rim=(
            np.concatenate([forward[MARGIN + TILE :], forward[:MARGIN]], 0),
            np.concatenate([stacked[:, :MARGIN], stacked[:, MARGIN + TILE :]], 1),
        ),
        q_own=(stacked[:, core],),
        spread=(np.block([[c_low, s_low], [-s_low, c_low]]),),
        q_low=(np.concatenate([c_low.T, s_low.T], 1), pad),
        interp=(high, interp - high),
        interp_t=(np.concatenate([high.T, (interp - high).T], 0),),
        gather=(
            np.block(
                [[c_low.T, -s_low.T, -s_low.T, -c_low.T], [s_low.T, c_low.T, c_low.T, -s_low.T]]
            ),
        ),
        q_back=(c_low, s_low),
        inv_left=(np.block([[c_core[:, HALF:], s_core[:, HALF:]], [-s_core[:, HALF:], c_core[:, HALF:]]]),),
        inv_right=(np.block([[c_core[:, :HALF], s_core[:, :HALF]], [-s_core[:, :HALF], c_core[:, :HALF]]]),),
        place=(place_a, place_b),
        q_place=(np.concatenate([place_a.T, place_b.T], 0),),
    )
    table = {name: np.concatenate(value, 1) for name, value in table.items()}
    starts = dict(zip(table, np.cumsum([0] + [len(value) for value in table.values()])))
    rows = {name: slice(int(starts[name]), int(starts[name]) + len(table[name])) for name in table}
    return np.concatenate(list(table.values()), 0).astype(jnp.bfloat16), rows


TABLE, TABLE_ROWS = tables()


class Tables:
    def __init__(self, ref):
        self.ref = ref

    def __getitem__(self, name):
        return self.ref[TABLE_ROWS[name], :]

    def left(self, name):
        return self.ref[TABLE_ROWS[name], :COARSE]

    def right(self, name):
        return self.ref[TABLE_ROWS[name], COARSE:]


def dot(left, right):
    return jnp.dot(left, right, preferred_element_type=F32)


def swap_halves(value):
    return pltpu.roll(value, MODES, axis=1)


def low_lanes(shape):
    return lax.broadcasted_iota(jnp.int32, shape, 1) < MODES


def modes_of(blocks):
    top, bottom = blocks[:MODES], swap_halves(blocks[MODES:])
    return jnp.where(low_lanes(top.shape), top - bottom, -(top + bottom)) / area


def imaging_modes(spec, goal, weight, modes_ref, weight_ref, field_ref, grad_ref, t):
    swapped = swap_halves(spec)
    low = low_lanes(spec.shape)
    spec_a = jnp.where(low, spec, swapped)
    spec_b = jnp.where(low, -swapped, spec)
    filtered = []
    for k in range(KERN):
        resp = modes_ref[k]
        filtered.append((resp * spec_a + swap_halves(resp) * spec_b).astype(BF16))
    partial = dot(jnp.concatenate(filtered, 0), t["spread"]).astype(BF16)
    level = jnp.zeros((COARSE, COARSE), F32)
    for k in range(KERN):
        part = partial[k * MODES : (k + 1) * MODES]
        real, imag = part[:, :COARSE], part[:, COARSE:]
        rotated = jnp.concatenate([part, jnp.concatenate([-imag, real], 1)], 0)
        field = dot(t.left("q_low"), rotated)
        field_ref[k] = field
        a_real, a_imag = field[:, :COARSE], field[:, COARSE:]
        level = level + weight_ref[k] * (a_real * a_real + a_imag * a_imag)
    level = level.astype(BF16)
    half = dot(t["interp"], jnp.concatenate([level, level], 0)).astype(BF16)
    core = dot(jnp.concatenate([half, half], 1), t["interp_t"])
    printed = jax.nn.sigmoid(steepness * (core - threshold))
    core_grad = 2.0 * (printed - goal.astype(F32)) * printed * (1.0 - printed) * steepness
    if weight is not None:
        core_grad = jnp.where(weight, core_grad, 0.0)
    low_grad = dot(t["interp_t"][:COARSE], core_grad.astype(BF16)).astype(BF16)
    low_grad = dot(low_grad, t.left("interp"))
    both = jnp.concatenate([low_grad, low_grad], 1)
    for k in range(KERN):
        scaled = field_ref[k] * both * (2.0 * weight_ref[k])
        grad_ref[k * COARSE : (k + 1) * COARSE, :] = scaled.astype(BF16)
    gathered = dot(grad_ref[...], t["gather"]).astype(BF16)
    direct = jnp.zeros((MODES, 2 * MODES), F32)
    crossed = jnp.zeros((MODES, 2 * MODES), F32)
    for k in range(KERN):
        rows = gathered[k * COARSE : (k + 1) * COARSE]
        back = dot(t["q_back"], jnp.concatenate([rows[:, :COARSE], rows[:, COARSE:]], 0))
        resp = modes_ref[k]
        direct = direct + resp * back
        crossed = crossed + swap_halves(resp) * back
    return jnp.where(low, direct + swap_halves(direct), crossed - swap_halves(crossed)).astype(BF16)


def edges_kernel(mask_ref, target_ref, edges_ref, left_ref):
    wire = jax.nn.sigmoid(mask_ref[...])
    edges = jnp.concatenate([wire[:, :MARGIN], wire[:, TILE - MARGIN :]], 1).astype(BF16)
    edges_ref[...] = edges
    left_ref[:, : 2 * MARGIN] = edges
    left_ref[:, 2 * MARGIN :] = target_ref[:, :HALF]


def strip_kernel(
    cols, mask_ref, target_ref, left_ref, right_ref, table_ref, u_ref, even_ref, odd_ref
):
    t = Tables(table_ref)
    col = lax.axis_index("col")
    odd = lax.rem(lax.axis_index("row"), 2) == 1
    wire = jax.nn.sigmoid(mask_ref[...]).astype(BF16)
    low = low_lanes((TILE, 2 * MARGIN))
    keep = jnp.logical_or(
        jnp.logical_and(low, col < cols - 1), jnp.logical_and(jnp.logical_not(low), col > 0)
    )
    rim = jnp.where(low, right_ref[:, : 2 * MARGIN].astype(F32), left_ref[...].astype(F32))
    rim = jnp.where(keep, rim, 0.0).astype(BF16)
    half_spec = (dot(wire, t.left("own")) + dot(rim, t.left("rim"))).astype(BF16)
    u_ref[...] = half_spec
    goals = jnp.concatenate([target_ref[:HALF, HALF:], right_ref[:HALF, 2 * MARGIN :]], 0)
    top, bottom = half_spec[:MARGIN], half_spec[TILE - MARGIN :]

    @pl.when(odd)
    def _():
        even_ref[:MARGIN, :] = top
        odd_ref[:MARGIN, :] = bottom

    @pl.when(jnp.logical_not(odd))
    def _():
        even_ref[:MARGIN, :] = bottom
        odd_ref[:MARGIN, :] = top

    even_ref[MARGIN:, :] = goals
    odd_ref[MARGIN:, :] = goals


def first_kernel(
    rows, mask_ref, u_ref, even_ref, odd_ref, goal_ref, modes_ref, weight_ref, table_ref,
    first_ref, aa_ref, ab_ref, ba_ref, bb_ref, field_ref, grad_ref,
):
    t = Tables(table_ref)
    row = lax.axis_index("row")
    odd = lax.rem(row, 2) == 1
    even_in, odd_in = even_ref[:MARGIN, :].astype(F32), odd_ref[:MARGIN, :].astype(F32)
    above = jnp.where(row > 0, jnp.where(odd, even_in, odd_in), 0.0)
    below = jnp.where(row < rows - 1, jnp.where(odd, odd_in, even_in), 0.0)
    rim = jnp.concatenate([above, below], 0).astype(BF16)
    spec = modes_of(dot(t["q_own"], u_ref[...]) + dot(t.right("rim"), rim))
    combined = imaging_modes(
        spec, goal_ref[...], None, modes_ref, weight_ref, field_ref, grad_ref, t
    )
    left = dot(combined, t["inv_right"]).astype(BF16)
    right = dot(combined, t["inv_left"]).astype(BF16)
    real = jnp.concatenate([left[:, :HALF], right[:, :HALF]], 1)
    imag = jnp.concatenate([left[:, HALF:], right[:, HALF:]], 1)
    mask_grad = dot(t.right("own"), jnp.concatenate([real, imag], 0)) / area
    mask = mask_ref[...]
    soft = jax.nn.sigmoid(mask)
    first = mask - step_rate * (mask_grad * soft * (1.0 - soft))
    first_ref[...] = first
    wire = jax.nn.sigmoid(first).astype(BF16)
    half = dot(wire, t["place"])
    half_hi = half.astype(BF16)
    half_lo = (half - half_hi.astype(F32)).astype(BF16)
    blocks = dot(t["q_place"], half_hi) + dot(t["q_place"], half_lo)
    aa_ref[...] = modes_of(blocks[:HALF, :HALF])
    ab_ref[...] = modes_of(blocks[:HALF, HALF:])
    ba_ref[...] = modes_of(blocks[HALF:, :HALF])
    bb_ref[...] = modes_of(blocks[HALF:, HALF:])


def heal_kernel(
    rows, cols, own_ref, right_ref, below_ref, corner_ref, goal_ref, goal_right_ref, even_ref,
    odd_ref, modes_ref, weight_ref, table_ref, out_ref, field_ref, grad_ref,
):
    row = lax.axis_index("row")
    inner_row = row < rows - 1
    inner_col = lax.axis_index("col") < cols - 1
    spec = own_ref[...]
    spec = spec + jnp.where(inner_col, right_ref[...], 0.0)
    spec = spec + jnp.where(inner_row, below_ref[...], 0.0)
    spec = spec + jnp.where(jnp.logical_and(inner_row, inner_col), corner_ref[...], 0.0)
    upper = jnp.concatenate([goal_ref[HALF:, HALF:], goal_right_ref[HALF:, HALF:]], 1)
    lower = jnp.where(
        lax.rem(row, 2) == 1, odd_ref[MARGIN:, :].astype(F32), even_ref[MARGIN:, :].astype(F32)
    )
    lower = jnp.concatenate([lower[:HALF], lower[HALF:]], 1)
    goal = jnp.concatenate([upper.astype(F32), lower], 0)
    shape = (TILE, TILE)
    weight = jnp.logical_and(
        jnp.logical_or(lax.broadcasted_iota(jnp.int32, shape, 0) < HALF, inner_row),
        jnp.logical_or(lax.broadcasted_iota(jnp.int32, shape, 1) < HALF, inner_col),
    )
    out_ref[...] = imaging_modes(
        spec, goal, weight, modes_ref, weight_ref, field_ref, grad_ref, Tables(table_ref)
    )


def final_kernel(first_ref, own_ref, left_ref, up_ref, corner_ref, table_ref, out_ref):
    t = Tables(table_ref)
    has_row = lax.axis_index("row") > 0
    has_col = lax.axis_index("col") > 0

    def kept(ref, flag):
        return jnp.where(flag, ref[...].astype(F32), 0.0).astype(BF16)

    left = jnp.concatenate(
        [kept(left_ref, has_col), kept(corner_ref, jnp.logical_and(has_row, has_col))], 0
    )
    right = jnp.concatenate([own_ref[...], kept(up_ref, has_row)], 0)
    left = dot(left, t["inv_left"]).astype(BF16)
    right = dot(right, t["inv_right"]).astype(BF16)

    def quarter(rows):
        real = jnp.concatenate([left[rows, :HALF], right[rows, :HALF]], 1)
        imag = jnp.concatenate([left[rows, HALF:], right[rows, HALF:]], 1)
        return jnp.concatenate([real, imag], 0)

    q_inv = t.right("own")
    lower = dot(q_inv[:HALF], quarter(slice(0, MODES)))
    upper = dot(q_inv[HALF:], quarter(slice(MODES, 2 * MODES)))
    grad = jnp.concatenate([upper, lower], 0) / area
    first = first_ref[...]
    soft = jax.nn.sigmoid(first)
    out_ref[...] = first - step_rate * (grad * soft * (1.0 - soft))


VMEM_SPEC = pl.BlockSpec(memory_space=VMEM)
SMEM_SPEC = pl.BlockSpec(memory_space=pltpu.SMEM)
FIELD_SCRATCH = [VMEM((KERN, COARSE, 2 * COARSE), F32), VMEM((KERN * COARSE, 2 * COARSE), BF16)]


def shape_of(rows, cols, dtype):
    return jax.ShapeDtypeStruct((rows, cols), dtype)


def per_device(rows, cols, mask_param, target, kernel_modes, kernel_weight):
    table = jnp.asarray(TABLE)

    def permuted(value, place):
        pairs = [
            (r * cols + c, place(r, c)[0] * cols + place(r, c)[1])
            for r in range(rows)
            for c in range(cols)
        ]
        return lax.ppermute(value, ("row", "col"), pairs)

    def move(value, down, right):
        return permuted(value, lambda r, c: ((r + down) % rows, (c + right) % cols))

    def swap(value, parity):
        def place(r, c):
            other = r + 1 if r % 2 == parity else r - 1
            return (other, c) if 0 <= other < rows else (r, c ^ 1)

        return permuted(value, place)

    def call(kernel, outs, smem, limit, scratch, name, *args):
        specs = [SMEM_SPEC if i in smem else VMEM_SPEC for i in range(len(args))]
        return pl.pallas_call(
            kernel, out_shape=outs, in_specs=specs,
            out_specs=jax.tree.map(lambda _: VMEM_SPEC, outs), scratch_shapes=scratch,
            compiler_params=pltpu.CompilerParams(vmem_limit_bytes=limit << 20), name=name,
        )(*args)

    edges, edges_left = call(
        edges_kernel, (shape_of(TILE, 2 * MARGIN, BF16), shape_of(TILE, TILE, BF16)),
        (), 4, (), "edges", mask_param, target,
    )
    from_left = move(edges, 0, 1)
    from_right = move(edges_left, 0, -1)
    rim_shape = shape_of(MARGIN + TILE, 2 * MODES, BF16)
    half_spec, even_rim, odd_rim = call(
        lambda *refs: strip_kernel(cols, *refs),
        (shape_of(TILE, 2 * MODES, BF16), rim_shape, rim_shape), (), 4, (), "strip",
        mask_param, target, from_left, from_right, table,
    )
    even_rim, odd_rim = swap(even_rim, 0), swap(odd_rim, 1)
    modes_shape = shape_of(MODES, 2 * MODES, F32)
    first, own, to_left, to_up, to_corner = call(
        lambda *refs: first_kernel(rows, *refs),
        (shape_of(TILE, TILE, F32),) + (modes_shape,) * 4, (6,), 12, FIELD_SCRATCH, "first",
        mask_param, half_spec, even_rim, odd_rim, target, kernel_modes, kernel_weight, table,
    )
    spec_right = move(to_left, 0, -1)
    spec_below = move(to_up, -1, 0)
    spec_corner = move(to_corner, -1, -1)
    combined = call(
        lambda *refs: heal_kernel(rows, cols, *refs),
        shape_of(MODES, 2 * MODES, BF16), (9,), 12, FIELD_SCRATCH, "heal",
        own, spec_right, spec_below, spec_corner, target, from_right, even_rim, odd_rim,
        kernel_modes, kernel_weight, table,
    )
    mode_left = move(combined, 0, 1)
    mode_up = move(combined, 1, 0)
    mode_corner = move(combined, 1, 1)
    return call(
        final_kernel, shape_of(TILE, TILE, F32), (), 4, (), "final",
        first, combined, mode_left, mode_up, mode_corner, table,
    )


def solution(mesh):
    rows, cols = mesh.shape["row"], mesh.shape["col"]
    tile = P(("grp", "row"), "col")
    return jax.shard_map(
        lambda *args: per_device(rows, cols, *args), mesh=mesh,
        in_specs=(tile, tile, P(), P()), out_specs=tile, check_vma=False,
    )
```

time: 48.6 us -> 35.6 us (0.73)
  Pallas kernels: 14.8 us -> 7.45 us
  starting transfers between devices: 16.9 us -> 11.7 us
  local copies, waits for them, and re-layouts: 5.28 us -> 3.15 us
  waiting for transfers between devices: 11.2 us -> 13 us
    pallas_call x5, Pallas kernels: 14.8 us -> 7.45 us  [call(): pl.pallas_call(kernel, out_shape=outs, in_specs=specs, out_specs=jax.tree...]
    ppermute x12 -> x10, starting transfers between devices: 16.9 us -> 11.7 us  [permuted(): return lax.ppermute(value, ('row', 'col'), pairs)]
    ppermute x12 -> x10, waiting for transfers between devices: 11.2 us -> 13 us  [permuted(): return lax.ppermute(value, ('row', 'col'), pairs)]
    slice x3 -> x0, local copies, waits for them, and re-layouts: 1.61 us -> none  [the longest x1 0.84 us: per_device(): goal_right = move(target[:, :HALF], 0, -1)]
    unnamed x24 -> x16, local copies, waits for them, and re-layouts: 3.67 us -> 3.15 us
  transfers between devices with their start and end apart: 12 -> 10, of which waited for: 6 -> 5; matrix products, arithmetic and copies ran while one was open for 2% -> 0% of each run, Pallas kernels for 18% -> 0%
where the time goes in v2:
time: 35.6 us; the launch traced here: 35.4 us
  waiting for transfers between devices  13 us (37%)
  starting transfers between devices  11.7 us (33%)
  Pallas kernels  7.45 us (21%)
  local copies, waits for them, and re-layouts  3.15 us (9%)
    ppermute x10, waiting for transfers between devices, permuted(): return lax.ppermute(value, ('row', 'col'), pairs)  13 us
    ppermute x10, starting transfers between devices, permuted(): return lax.ppermute(value, ('row', 'col'), pairs)  11.7 us
    pallas_call x5, Pallas kernels, call(): pl.pallas_call(kernel, out_shape=outs, in_specs=specs, out_specs=jax.tree...  7.45 us
    unnamed x16, local copies, waits for them, and re-layouts  3.15 us
  transfers between devices with their start and end apart: 10, of which 5 were waited for; matrix products, arithmetic and copies ran while one was open for 0% of the time, Pallas kernels for 0%

profile of v2, /device:TPU:0, one launch (start us, length us, event | category | flops | bytes accessed | tf_op | source)
XLA Modules:
  0.0 35.4 jit_solution(6052108749517382166)
XLA Ops:
  0.0 0.0 copy-start.2
  0.0 0.9 %copy-done.2 = f32[256,256]{1,0:T(8,128)S(1)} copy-done((f32[256,256]{1,0:T(8,128)S(1)}, f32[256,256]{1,0:T(8,128)}, u32[]{:S(2)}) %copy-start.2) | copy-done | bytes 262168
  1.0 0.0 copy-start.4
  1.0 0.9 %copy-done.4 = bf16[256,256]{1,0:T(8,128)(2,1)S(1)} copy-done((bf16[256,256]{1,0:T(8,128)(2,1)S(1)}, bf16[256,256]{1,0:T(8,128)(2,1)}, u32[]{:S(2)}) %copy-start.4) | copy-done | bytes 131096
  1.9 0.0 copy-start.3
  1.9 0.0 copy-start.5
  1.9 0.0 copy-start.7
  1.9 2.5 %collective-permute-start.1 = (bf16[256,256]{1,0:T(8,128)(2,1)S(1)}, bf16[256,256]{1,0:T(8,128)(2,1)S(1)}, u32[]{:S(2)}, u32[]{:S(2)}) collective-permute-start(bf16[256,256]{1,0:T(8,128)(2,1)S(1)} %get-tuple-element.16), channel_id=1, source_target_pairs={{0,3},{1,0},{2,1},{3,2},{4,7},{5,4},{6,5},{7,6},{8,11},{9,8},{10,9... | collective-permute-start | bytes 393224 | tf_op jit(solution)/shard_map/ppermute | solution.py:305
  4.4 0.0 collective-permute-start
  4.4 4.2 %collective-permute-done.refs_2_ = bf16[256,128]{1,0:T(8,128)(2,1)S(1)} collective-permute-done((bf16[256,128]{1,0:T(8,128)(2,1)S(1)}, bf16[256,128]{1,0:T(8,128)(2,1)S(1)}, u32[]{:S(2)}, u32[]{:S(2)}) %collective-permute-start) | collective-permute-done | bytes 65568 | tf_op jit(solution)/shard_map/ppermute | solution.py:305
  8.6 0.0 collective-permute-done.1.refs_3_.refs_5_
  8.6 0.0 copy-start
  8.6 1.3 %copy-done = bf16[2368,256]{1,0:T(8,128)(2,1)S(1)} copy-done((bf16[2368,256]{1,0:T(8,128)(2,1)S(1)}, bf16[2368,256]{1,0:T(8,128)(2,1)}, u32[]{:S(2)}) %copy-start) | copy-done | bytes 1212440
  9.9 0.0 copy-start.1
  9.9 0.0 copy-start.6
  9.9 0.2 strip.1
  10.1 1.6 %collective-permute-start.2 = (bf16[320,128]{1,0:T(8,128)(2,1)S(1)}, bf16[320,128]{1,0:T(8,128)(2,1)S(1)}, u32[]{:S(2)}, u32[]{:S(2)}) collective-permute-start(bf16[320,128]{1,0:T(8,128)(2,1)S(1)} %get-tuple-element.18), channel_id=1, source_target_pairs={{0,4},{1,5},{2,6},{3,7},{4,0},{5,1},{6,2},{7,3},{8,12},{9,13},{10,... | collective-permute-start | bytes 245768 | tf_op jit(solution)/shard_map/ppermute | solution.py:305
  11.7 0.0 collective-permute-start.3
  11.7 2.9 %collective-permute-done.2.refs_2_.refs_6_ = bf16[320,128]{1,0:T(8,128)(2,1)S(1)} collective-permute-done((bf16[320,128]{1,0:T(8,128)(2,1)S(1)}, bf16[320,128]{1,0:T(8,128)(2,1)S(1)}, u32[]{:S(2)}, u32[]{:S(2)}) %collective-permute-start.2) | collective-permute-done | bytes 81952 | tf_op jit(solution)/shard_map/ppermute | solution.py:305
  14.6 0.0 collective-permute-done.3.refs_3_.refs_7_
  14.6 0.0 copy-done.3
  14.6 0.0 copy-done.5
  14.6 0.0 copy-done.7
  14.6 0.0 copy-done.1
  14.6 0.0 copy-done.6
  14.6 3.5 %first.1 = (f32[256,256]{1,0:T(8,128)S(1)}, f32[64,128]{1,0:T(8,128)S(1)}, f32[64,128]{1,0:T(8,128)S(1)}, f32[64,128]{1,0:T(8,128)S(1)}, f32[64,128]{1,0:T(8,128)S(1)}) custom-call(f32[256,256]{1,0:T(8,128)S(1)} %copy-done.3, bf16[256,128]{1,0:T(8,128)(2,1)S(1)} %get-tuple-element.17.refs_1_, bf16[320,128]{1,0:T(8,128)(2,1)S(1)} %collective-permute-done.2.refs_2_.refs_6_, ...), custom_call_target="tpu_custom_call" | custom-call | tf_op jit(solution)/shard_map/first/pallas_call | solution.py:319
  18.2 0.5 %collective-permute-start.4 = (f32[64,128]{1,0:T(8,128)S(1)}, f32[64,128]{1,0:T(8,128)S(1)}, u32[]{:S(2)}, u32[]{:S(2)}) collective-permute-start(f32[64,128]{1,0:T(8,128)S(1)} %get-tuple-element.22), channel_id=1, source_target_pairs={{0,3},{1,0},{2,1},{3,2},{4,7},{5,4},{6,5},{7,6},{8,11},{9,8},{10,9... | collective-permute-start | bytes 98312 | tf_op jit(solution)/shard_map/ppermute | solution.py:305
  18.6 3.6 %collective-permute-start.5 = (f32[64,128]{1,0:T(8,128)S(1)}, f32[64,128]{1,0:T(8,128)S(1)}, u32[]{:S(2)}, u32[]{:S(2)}) collective-permute-start(f32[64,128]{1,0:T(8,128)S(1)} %get-tuple-element.23), channel_id=1, source_target_pairs={{0,12},{1,13},{2,14},{3,15},{4,0},{5,1},{6,2},{7,3},{8,4},{9,5},{1... | collective-permute-start | bytes 98312 | tf_op jit(solution)/shard_map/ppermute | solution.py:305
  22.3 1.8 %collective-permute-start.6 = (f32[64,128]{1,0:T(8,128)S(1)}, f32[64,128]{1,0:T(8,128)S(1)}, u32[]{:S(2)}, u32[]{:S(2)}) collective-permute-start(f32[64,128]{1,0:T(8,128)S(1)} %get-tuple-element.24), channel_id=1, source_target_pairs={{0,15},{1,12},{2,13},{3,14},{4,3},{5,0},{6,1},{7,2},{8,7},{9,4},{1... | collective-permute-start | bytes 98312 | tf_op jit(solution)/shard_map/ppermute | solution.py:305
  24.0 0.0 collective-permute-done.4.refs_1_
  24.1 0.0 collective-permute-done.5.refs_2_
  24.1 1.6 %collective-permute-done.6.refs_3_ = f32[64,128]{1,0:T(8,128)S(1)} collective-permute-done((f32[64,128]{1,0:T(8,128)S(1)}, f32[64,128]{1,0:T(8,128)S(1)}, u32[]{:S(2)}, u32[]{:S(2)}) %collective-permute-start.6) | collective-permute-done | bytes 32800 | tf_op jit(solution)/shard_map/ppermute | solution.py:305
  25.6 2.6 %heal.1.own_ref = bf16[64,128]{1,0:T(8,128)(2,1)S(1)} custom-call(f32[64,128]{1,0:T(8,128)S(1)} %get-tuple-element.21.refs_0_, f32[64,128]{1,0:T(8,128)S(1)} %collective-permute-done.4.refs_1_, f32[64,128]{1,0:T(8,128)S(1)} %collective-permute-done.5.refs_2_, f32[64,128]{1,0:T(8,128)S(1)} %collective-permute-done.6.refs_3_, bf16[256,256]{1,0:T(8,128)(2,1)S(1)} %copy-done.5, ...), custom_call_target="tpu_custom_call" | custom-call | tf_op jit(solution)/shard_map/heal/pallas_call | solution.py:319
  28.2 0.1 collective-permute-start.9
  28.3 1.7 %collective-permute-start.8 = (bf16[64,128]{1,0:T(8,128)(2,1)S(1)}, bf16[64,128]{1,0:T(8,128)(2,1)S(1)}, u32[]{:S(2)}, u32[]{:S(2)}) collective-permute-start(bf16[64,128]{1,0:T(8,128)(2,1)S(1)} %heal.1.own_ref), channel_id=1, source_target_pairs={{0,4},{1,5},{2,6},{3,7},{4,8},{5,9},{6,10},{7,11},{8,12},{9,13},{1... | collective-permute-start | bytes 49160 | tf_op jit(solution)/shard_map/ppermute | solution.py:305
  30.0 0.0 collective-permute-start.7
  30.0 4.2 %collective-permute-done.9.corner_ref = bf16[64,128]{1,0:T(8,128)(2,1)S(1)} collective-permute-done((bf16[64,128]{1,0:T(8,128)(2,1)S(1)}, bf16[64,128]{1,0:T(8,128)(2,1)S(1)}, u32[]{:S(2)}, u32[]{:S(2)}) %collective-permute-start.9) | collective-permute-done | bytes 16416 | tf_op jit(solution)/shard_map/ppermute | solution.py:305
  34.2 0.2 collective-permute-done.8.up_ref
  34.3 0.0 collective-permute-done.7.left_ref
  34.3 1.0 %final.1 = f32[256,256]{1,0:T(8,128)} custom-call(f32[256,256]{1,0:T(8,128)S(1)} %get-tuple-element.20.first_ref, bf16[64,128]{1,0:T(8,128)(2,1)S(1)} %heal.1.own_ref, bf16[64,128]{1,0:T(8,128)(2,1)S(1)} %collective-permute-done.7.left_ref, bf16[64,128]{1,0:T(8,128)(2,1)S(1)} %collective-permute-done.8.up_ref, ...), custom_call_target="tpu_custom_call" | custom-call | tf_op jit(solution)/shard_map/final/pallas_call | solution.py:319
  (1 shorter events, 0.0 us)
Async XLA Ops:
  0.0 0.9 %copy-start.2 = (f32[256,256]{1,0:T(8,128)S(1)}, f32[256,256]{1,0:T(8,128)}, u32[]{:S(2)}) copy-start(f32[256,256]{1,0:T(8,128)} %refs_0_.3) | copy-start | bytes 786436
  1.0 0.9 %copy-start.4 = (bf16[256,256]{1,0:T(8,128)(2,1)S(1)}, bf16[256,256]{1,0:T(8,128)(2,1)}, u32[]{:S(2)}) copy-start(bf16[256,256]{1,0:T(8,128)(2,1)} %refs_4_.4) | copy-start | bytes 393220
  1.9 12.8 %copy-start.3 = (f32[256,256]{1,0:T(8,128)S(1)}, f32[256,256]{1,0:T(8,128)}, u32[]{:S(2)}) copy-start(f32[256,256]{1,0:T(8,128)} %refs_0_.3) | copy-start | bytes 786436
  1.9 12.8 %copy-start.5 = (bf16[256,256]{1,0:T(8,128)(2,1)S(1)}, bf16[256,256]{1,0:T(8,128)(2,1)}, u32[]{:S(2)}) copy-start(bf16[256,256]{1,0:T(8,128)(2,1)} %refs_4_.4) | copy-start | bytes 393220
  1.9 12.8 %copy-start.7 = (f32[12]{0:T(128)S(1)}, f32[12]{0:T(128)}, u32[]{:S(2)}) copy-start(f32[12]{0:T(128)} %refs_9_.1) | copy-start | bytes 148
  1.9 6.7 %collective-permute-start.1 = (bf16[256,256]{1,0:T(8,128)(2,1)S(1)}, bf16[256,256]{1,0:T(8,128)(2,1)S(1)}, u32[]{:S(2)}, u32[]{:S(2)}) collective-permute-start(bf16[256,256]{1,0:T(8,128)(2,1)S(1)} %get-tuple-element.16), channel_id=1, source_target_pairs={{0,3},{1,0},{2,1},{3,2},{4,7},{5,4},{6,5},{7,6},{8,11},{9,8},{10,9... | collective-permute-start | bytes 393224 | tf_op jit(solution)/shard_map/ppermute | solution.py:305
  4.4 4.2 %collective-permute-start = (bf16[256,128]{1,0:T(8,128)(2,1)S(1)}, bf16[256,128]{1,0:T(8,128)(2,1)S(1)}, u32[]{:S(2)}, u32[]{:S(2)}) collective-permute-start(bf16[256,128]{1,0:T(8,128)(2,1)S(1)} %get-tuple-element.15), channel_id=1, source_target_pairs={{0,1},{1,2},{2,3},{3,0},{4,5},{5,6},{6,7},{7,4},{8,9},{9,10},{10,1... | collective-permute-start | bytes 196616 | tf_op jit(solution)/shard_map/ppermute | solution.py:305
  8.6 1.3 %copy-start = (bf16[2368,256]{1,0:T(8,128)(2,1)S(1)}, bf16[2368,256]{1,0:T(8,128)(2,1)}, u32[]{:S(2)}) copy-start(bf16[2368,256]{1,0:T(8,128)(2,1)} %constant.2.clone.refs_4_.refs_7_.refs_10_.table_ref) | copy-start | bytes 3637252
  9.9 4.8 %copy-start.1 = (bf16[2368,256]{1,0:T(8,128)(2,1)S(1)}, bf16[2368,256]{1,0:T(8,128)(2,1)}, u32[]{:S(2)}) copy-start(bf16[2368,256]{1,0:T(8,128)(2,1)} %constant.2.clone.refs_4_.refs_7_.refs_10_.table_ref) | copy-start | bytes 3637252
  9.9 4.8 %copy-start.6 = (f32[12,64,128]{2,1,0:T(8,128)S(1)}, f32[12,64,128]{2,1,0:T(8,128)}, u32[]{:S(2)}) copy-start(f32[12,64,128]{2,1,0:T(8,128)} %refs_8_.1) | copy-start | bytes 1179652
  10.1 4.5 %collective-permute-start.2 = (bf16[320,128]{1,0:T(8,128)(2,1)S(1)}, bf16[320,128]{1,0:T(8,128)(2,1)S(1)}, u32[]{:S(2)}, u32[]{:S(2)}) collective-permute-start(bf16[320,128]{1,0:T(8,128)(2,1)S(1)} %get-tuple-element.18), channel_id=1, source_target_pairs={{0,4},{1,5},{2,6},{3,7},{4,0},{5,1},{6,2},{7,3},{8,12},{9,13},{10,... | collective-permute-start | bytes 245768 | tf_op jit(solution)/shard_map/ppermute | solution.py:305
  11.7 2.9 %collective-permute-start.3 = (bf16[320,128]{1,0:T(8,128)(2,1)S(1)}, bf16[320,128]{1,0:T(8,128)(2,1)S(1)}, u32[]{:S(2)}, u32[]{:S(2)}) collective-permute-start(bf16[320,128]{1,0:T(8,128)(2,1)S(1)} %get-tuple-element.19), channel_id=1, source_target_pairs={{0,1},{1,0},{2,3},{3,2},{4,8},{5,9},{6,10},{7,11},{8,4},{9,5},{10,... | collective-permute-start | bytes 245768 | tf_op jit(solution)/shard_map/ppermute | solution.py:305
  18.2 5.9 %collective-permute-start.4 = (f32[64,128]{1,0:T(8,128)S(1)}, f32[64,128]{1,0:T(8,128)S(1)}, u32[]{:S(2)}, u32[]{:S(2)}) collective-permute-start(f32[64,128]{1,0:T(8,128)S(1)} %get-tuple-element.22), channel_id=1, source_target_pairs={{0,3},{1,0},{2,1},{3,2},{4,7},{5,4},{6,5},{7,6},{8,11},{9,8},{10,9... | collective-permute-start | bytes 98312 | tf_op jit(solution)/shard_map/ppermute | solution.py:305
  18.6 5.4 %collective-permute-start.5 = (f32[64,128]{1,0:T(8,128)S(1)}, f32[64,128]{1,0:T(8,128)S(1)}, u32[]{:S(2)}, u32[]{:S(2)}) collective-permute-start(f32[64,128]{1,0:T(8,128)S(1)} %get-tuple-element.23), channel_id=1, source_target_pairs={{0,12},{1,13},{2,14},{3,15},{4,0},{5,1},{6,2},{7,3},{8,4},{9,5},{1... | collective-permute-start | bytes 98312 | tf_op jit(solution)/shard_map/ppermute | solution.py:305
  22.3 3.4 %collective-permute-start.6 = (f32[64,128]{1,0:T(8,128)S(1)}, f32[64,128]{1,0:T(8,128)S(1)}, u32[]{:S(2)}, u32[]{:S(2)}) collective-permute-start(f32[64,128]{1,0:T(8,128)S(1)} %get-tuple-element.24), channel_id=1, source_target_pairs={{0,15},{1,12},{2,13},{3,14},{4,3},{5,0},{6,1},{7,2},{8,7},{9,4},{1... | collective-permute-start | bytes 98312 | tf_op jit(solution)/shard_map/ppermute | solution.py:305
  28.2 5.9 %collective-permute-start.9 = (bf16[64,128]{1,0:T(8,128)(2,1)S(1)}, bf16[64,128]{1,0:T(8,128)(2,1)S(1)}, u32[]{:S(2)}, u32[]{:S(2)}) collective-permute-start(bf16[64,128]{1,0:T(8,128)(2,1)S(1)} %heal.1.own_ref), channel_id=1, source_target_pairs={{0,5},{1,6},{2,7},{3,4},{4,9},{5,10},{6,11},{7,8},{8,13},{9,14},{1... | collective-permute-start | bytes 49160 | tf_op jit(solution)/shard_map/ppermute | solution.py:305
  28.3 6.0 %collective-permute-start.8 = (bf16[64,128]{1,0:T(8,128)(2,1)S(1)}, bf16[64,128]{1,0:T(8,128)(2,1)S(1)}, u32[]{:S(2)}, u32[]{:S(2)}) collective-permute-start(bf16[64,128]{1,0:T(8,128)(2,1)S(1)} %heal.1.own_ref), channel_id=1, source_target_pairs={{0,4},{1,5},{2,6},{3,7},{4,8},{5,9},{6,10},{7,11},{8,12},{9,13},{1... | collective-permute-start | bytes 49160 | tf_op jit(solution)/shard_map/ppermute | solution.py:305
  30.0 4.4 %collective-permute-start.7 = (bf16[64,128]{1,0:T(8,128)(2,1)S(1)}, bf16[64,128]{1,0:T(8,128)(2,1)S(1)}, u32[]{:S(2)}, u32[]{:S(2)}) collective-permute-start(bf16[64,128]{1,0:T(8,128)(2,1)S(1)} %heal.1.own_ref), channel_id=1, source_target_pairs={{0,1},{1,2},{2,3},{3,0},{4,5},{5,6},{6,7},{7,4},{8,9},{9,10},{10,1... | collective-permute-start | bytes 49160 | tf_op jit(solution)/shard_map/ppermute | solution.py:305
